TPU v7x, 128 devices: a whole 4x4x4 slice. The times are simulated.
128 devices in a mesh: group: 4 (over y_hi, core), member: 32 (over x, y_lo, z).
Axes of the slice: x: 4, y: 4 (y_hi: 2, y_lo: 2; y = y_hi * 2 + y_lo), z: 4, core: 2. Of those that a mesh axis runs over, the one named last changes fastest.
Arguments:
- face_schur: float32 [512, 6, 256, 256], P(('group', 'member')), as said below
- face_inverse: float32 [512, 6, 256, 256], P(('group', 'member')), as said below
- face_basis: float32 [512, 6, 96, 256], P(('group', 'member')), may hold values from -6 to 6
- partner: int32 [512, 6], P(('group', 'member')), may hold values from 0 to 3071, as said below
- prim_index: int32 [512, 96], P(('group', 'member')), may hold values from 0 to 24575
Outputs:
- deluxe_basis: float32 [512, 6, 96, 256], P(('group', 'member'))
- coarse_blocks: float32 [512, 9216], P('group')
Inputs may be any that keep to these rules, and one draw needn't show every extreme that they name: partner pairs the faces: the partner of the partner of a face is the face itself; a face of subdomain s has its partner on another device of the same group, where subdomain s lies on device s // 4 and devices k * 32 to (k + 1) * 32 - 1 form group k; at most 1 faces of one device have partners on one other device, and some pair of devices has exactly 1. Every block of face_schur is exactly symmetric and positive definite. Every block of face_inverse is exactly symmetric.
All inputs are finite; a program needn't handle non-finite values.
Results may differ from a plain program's by a relative error of at most 0.0003.
Values sent between devices are 32-bit elements; how exact they have to be, the bound alone decides.
No kernel may reach another device: no remote copies, remote signals or barrier semaphores. Data moves between devices by JAX's collectives and lax.ppermute only.
A program may use at most 128 MiB of HBM per device.

v0:
```python
import jax
import jax.numpy as jnp
from jax import lax
from jax.sharding import PartitionSpec as P

SWEEPS = 2
COARSE_PER_SUB = 48


FULL_PRECISION = lax.Precision.HIGHEST


def inverse_sweeps(summed, initial):
    doubled = 2.0 * jnp.eye(summed.shape[-1], dtype=jnp.float32)
    current = initial
    for repeat in range(SWEEPS):
        applied = jnp.einsum("fij,fjk->fik", summed, current, precision=FULL_PRECISION)
        current = jnp.einsum("fij,fjk->fik", current, doubled - applied, precision=FULL_PRECISION)
    return current


def face_terms(own_schur, other_schur, own_inverse, other_inverse, basis):
    summed = own_schur + other_schur
    approx_inverse = inverse_sweeps(summed, 0.25 * (own_inverse + other_inverse))
    product = jnp.einsum("fck,fjk->fcj", basis, own_schur, precision=FULL_PRECISION)
    deluxe = jnp.einsum("fck,fik->fci", product, approx_inverse, precision=FULL_PRECISION)
    weighted = jnp.einsum("fci,fij->fcj", deluxe, other_schur, precision=FULL_PRECISION)
    face_block = jnp.einsum("fcj,fdj->fcd", weighted, deluxe, precision=FULL_PRECISION)
    return (deluxe, face_block)


def assemble_diagonal(local_diagonal):
    return lax.psum(local_diagonal, ("group", "member"))


def local(face_schur, face_inverse, face_basis, partner, prim_index):
    sub_count = face_schur.shape[0]
    face_width = face_schur.shape[-1]
    prim_count = face_basis.shape[2]
    face_count = sub_count * 6
    members = lax.axis_size("member")
    groups = lax.axis_size("group")
    capacity = (face_count + members - 2) // (members - 1)
    own_schur = face_schur.reshape(face_count, face_width, face_width)
    own_inverse = face_inverse.reshape(face_count, face_width, face_width)
    basis = face_basis.reshape(face_count, prim_count, face_width)
    targets = partner.reshape(face_count)
    target_member = targets // face_count % members
    target_local = targets % face_count
    same_peer = target_member[:, None] == target_member[None, :]
    order_index = jnp.arange(face_count, dtype=jnp.int32)
    send_rank = jnp.sum(same_peer & (order_index[None, :] < order_index[:, None]), axis=1)
    recv_rank = jnp.sum(same_peer & (target_local[None, :] < target_local[:, None]), axis=1)
    stacked = jnp.stack([own_schur, own_inverse], axis=1)
    buffer = (
        jnp.zeros((members, capacity) + stacked.shape[1:], jnp.float32)
        .at[target_member, send_rank]
        .set(stacked)
    )
    received = lax.all_to_all(buffer, "member", split_axis=0, concat_axis=0, tiled=True)
    picked = received[target_member, recv_rank]
    deluxe, face_block = face_terms(own_schur, picked[:, 0], own_inverse, picked[:, 1], basis)
    galerkin = jnp.sum(face_block.reshape(sub_count, 6, prim_count, prim_count), axis=1)
    diagonal_terms = jnp.diagonal(galerkin, axis1=1, axis2=2)
    coarse_total = COARSE_PER_SUB * sub_count * groups * members
    local_diagonal = (
        jnp.zeros((coarse_total,), jnp.float32)
        .at[prim_index.reshape(-1)]
        .add(diagonal_terms.reshape(-1))
    )
    assembled = assemble_diagonal(local_diagonal)
    scales = 1.0 / jnp.sqrt(assembled[prim_index])
    scaled = scales[:, :, None] * galerkin * scales[:, None, :]
    coarse_blocks = lax.all_gather(
        scaled.reshape(sub_count, prim_count * prim_count), "member", axis=0, tiled=True
    )
    deluxe_basis = deluxe.reshape(sub_count, 6, prim_count, face_width)
    return (deluxe_basis, coarse_blocks)


def solution(mesh):
    in_specs = (
        P(("group", "member"), None, None, None),
        P(("group", "member"), None, None, None),
        P(("group", "member"), None, None, None),
        P(("group", "member"), None),
        P(("group", "member"), None),
    )
    out_specs = (P(("group", "member"), None, None, None), P("group", None))
    return jax.shard_map(local, mesh=mesh, in_specs=in_specs, out_specs=out_specs, check_vma=False)
```

profile of v0, /device:TPU:0, one launch (start us, length us, event | category | flops | bytes accessed | tf_op | source)
XLA Modules:
  0.0 754.7 jit_solution(1772734053315307162)
XLA Ops:
  9.4 10.6 %pad_maximum_fusion = f32[24,2,256,256]{3,2,1,0:T(8,128)} fusion(f32[24,1,256,256]{3,2,1,0:T(8,128)} %bitcast.62, f32[24,1,256,256]{3,2,1,0:T(8,128)} %bitcast.58), kind=kLoop, calls=%fused_computation.5 | loop fusion | flops 3145728 | bytes 25165824 | tf_op jit(solution)/shard_map/stack | solution.py:54
  20.0 7.8 %broadcast.301 = f32[32,2,256,256]{3,2,1,0:T(8,128)} broadcast(f32[]{:T(128)} %constant.47.clone.1), dimensions={} | broadcast | bytes 16777220 | tf_op jit(solution)/shard_map/broadcast_in_dim | solution.py:56
  27.7 23.0 %scatter_fusion = f32[32,2,256,256]{3,2,1,0:T(8,128)} fusion(f32[32,2,256,256]{3,2,1,0:T(8,128)} %broadcast.301, s32[24]{0:T(128)S(1)} %fusion.24, f32[24,2,256,256]{3,2,1,0:T(8,128)} %pad_maximum_fusion), kind=kCustom, calls=%fused_computation.3 | custom fusion | bytes 37748832 | tf_op jit(solution)/shard_map/scatter | solution.py:58
  50.7 9.4 %all-to-all-start = ((f32[32,1,2,256,256]{4,3,2,1,0:T(8,128)}), f32[32,1,2,256,256]{4,3,2,1,0:T(8,128)}, u32[]{:S(2)}, u32[]{:S(2)}) async-start(f32[32,1,2,256,256]{4,3,2,1,0:T(8,128)} %bitcast.57), calls=%async_computation | async-start | bytes 33554432 | tf_op jit(solution)/shard_map/all_to_all | solution.py:60
  60.5 10.1 %fusion.25 = f32[24,96,256]{2,1,0:T(8,128)} fusion(f32[24,96,256]{2,1,0:T(8,128)S(1)} %bitcast.56, f32[24,256,256]{2,1,0:T(8,128)} %bitcast.59), kind=kOutput, calls=%fused_computation.59 | convolution fusion | flops 1811939328 | bytes 11010048 | tf_op jit(solution)/shard_map/fck,fjk->fcj/dot_general | solution.py:25
  70.6 256.8 %all-to-all-done = f32[32,1,2,256,256]{4,3,2,1,0:T(8,128)} async-done(((f32[32,1,2,256,256]{4,3,2,1,0:T(8,128)}), f32[32,1,2,256,256]{4,3,2,1,0:T(8,128)}, u32[]{:S(2)}, u32[]{:S(2)}) %all-to-all-start) | async-done | bytes 16777248 | tf_op jit(solution)/shard_map/all_to_all | solution.py:60
  327.4 13.1 %gather_fusion = f32[24,2,256,256]{3,2,1,0:T(8,128)} fusion(f32[32,1,2,256,256]{4,3,2,1,0:T(8,128)} %all-to-all-done, s32[24]{0:T(128)S(1)} %get-tuple-element.4), kind=kCustom, calls=%fused_computation | custom fusion | bytes 25166016 | tf_op jit(solution)/shard_map/gather | solution.py:61
  340.5 9.0 %fusion.1 = f32[24,256,256]{2,1,0:T(8,128)} fusion(f32[24,2,256,256]{3,2,1,0:T(8,128)} %gather_fusion, f32[4,6,256,256]{3,2,1,0:T(8,128)} %param.6), kind=kLoop, calls=%fused_computation.9 | loop fusion | flops 3145728 | bytes 18874368 | tf_op jit(solution)/shard_map/mul | solution.py:24
  349.6 1.4 copy-done.2
  351.0 13.8 %fusion.12 = f32[24,256,256]{2,1,0:T(8,128)} fusion(f32[24,256,256]{2,1,0:T(8,128)} %fusion.1, f32[24,256,256]{2,1,0:T(8,128)} %bitcast.60, f32[24,2,256,256]{3,2,1,0:T(8,128)S(1)} %copy-done.2), kind=kOutput, calls=%fused_computation.19 | convolution fusion | flops 4833411072 | bytes 25165824 | tf_op jit(solution)/shard_map/fij,fjk->fik/dot_general | solution.py:17
  364.8 14.0 %fusion.4 = f32[24,256,256]{2,1,0:T(8,128)} fusion(f32[24,256,256]{2,1,0:T(8,128)} %fusion.1, f32[24,256,256]{2,1,0:T(8,128)} %fusion.12, f32[256,256]{1,0:T(8,128)S(1)} %fusion.14), kind=kOutput, calls=%fused_computation.12 | convolution fusion | flops 4833411072 | bytes 19136512 | tf_op jit(solution)/shard_map/fij,fjk->fik/dot_general | solution.py:18
  378.8 14.0 %fusion.10 = f32[24,256,256]{2,1,0:T(8,128)} fusion(f32[24,256,256]{2,1,0:T(8,128)} %fusion.4, f32[24,256,256]{2,1,0:T(8,128)} %bitcast.61, f32[24,2,256,256]{3,2,1,0:T(8,128)S(1)} %copy-done.2), kind=kOutput, calls=%fused_computation.18 | convolution fusion | flops 4833411072 | bytes 25165824 | tf_op jit(solution)/shard_map/fij,fjk->fik/dot_general | solution.py:17
  392.9 12.8 %fusion.2 = f32[24,256,256]{2,1,0:T(8,128)S(1)} fusion(f32[24,256,256]{2,1,0:T(8,128)} %fusion.4, f32[24,256,256]{2,1,0:T(8,128)} %fusion.10, f32[256,256]{1,0:T(8,128)S(1)} %fusion.14), kind=kOutput, calls=%fused_computation.10 | convolution fusion | flops 4833411072 | bytes 19136512 | tf_op jit(solution)/shard_map/fij,fjk->fik/dot_general | solution.py:18
  405.7 5.9 fusion.26
  411.6 4.2 fusion.6
  415.9 2.4 fusion.27
  418.4 3.2 copy.25
  421.7 2.9 gather_fusion.1
  424.8 3.9 scatter_custom_fusion.1
  428.7 151.2 %all-reduce.2.cloned.1.call-done = f32[24576]{0:T(1024)} async-done(((f32[24576]{0:T(1024)}), f32[24576]{0:T(1024)}) %all-reduce.2.cloned.1.call-update) | async-done | bytes 98320 | tf_op jit(solution)/shard_map/psum | solution.py:33
  579.9 3.6 gather_fusion.2
  583.6 1.1 multiply_multiply_fusion
  585.5 156.2 %all-gather.3.cloned.1.call-done = f32[32,4,9216]{2,1,0:T(4,128)} async-done(((f32[1,4,9216]{2,1,0:T(4,128)}), f32[32,4,9216]{2,1,0:T(4,128)}) %all-gather.3.cloned.1.call-update) | async-done | bytes 4718608 | tf_op jit(solution)/shard_map/all_gather | solution.py:74
  741.7 5.6 reshape.301
  (41 shorter events, 3.7 us)
Async XLA Ops:
  7.2 53.3 %copy-start = (f32[4,6,96,256]{3,2,1,0:T(8,128)S(1)}, f32[4,6,96,256]{3,2,1,0:T(8,128)}, u32[]{:S(2)}) copy-start(f32[4,6,96,256]{3,2,1,0:T(8,128)} %param.7) | copy-start | bytes 7077892
  50.7 9.5 %copy-start.6 = (s32[4,96]{1,0:T(4,128)S(1)}, s32[4,96]{1,0:T(4,128)}, u32[]{:S(2)}) copy-start(s32[4,96]{1,0:T(4,128)} %param.9) | copy-start | bytes 4612
  50.7 276.7 %all-to-all-start = ((f32[32,1,2,256,256]{4,3,2,1,0:T(8,128)}), f32[32,1,2,256,256]{4,3,2,1,0:T(8,128)}, u32[]{:S(2)}, u32[]{:S(2)}) async-start(f32[32,1,2,256,256]{4,3,2,1,0:T(8,128)} %bitcast.57), calls=%async_computation | async-start | bytes 33554432 | tf_op jit(solution)/shard_map/all_to_all | solution.py:60
  60.2 519.8 %all-reduce.2.cloned.1.call-start = ((), (), s32[]{:S(2)}) async-start(), calls=%async_computation.1 | async-start | bytes 196608 | tf_op jit(solution)/shard_map/psum | solution.py:33
  340.5 10.5 %copy-start.2 = (f32[24,2,256,256]{3,2,1,0:T(8,128)S(1)}, f32[24,2,256,256]{3,2,1,0:T(8,128)}, u32[]{:S(2)}) copy-start(f32[24,2,256,256]{3,2,1,0:T(8,128)} %gather_fusion) | copy-start | bytes 37748740
  392.9 12.8 %copy-start.4 = (f32[24,96,256]{2,1,0:T(8,128)S(1)}, f32[24,96,256]{2,1,0:T(8,128)}, u32[]{:S(2)}) copy-start(f32[24,96,256]{2,1,0:T(8,128)} %fusion.25) | copy-start | bytes 7077892
  411.6 6.7 copy-start.3
  418.4 6.2 copy-start.5
  424.8 322.6 %copy-start.1 = (f32[4,6,96,256]{3,2,1,0:T(8,128)S(1)}, f32[4,6,96,256]{3,2,1,0:T(8,128)}, u32[]{:S(2)}) copy-start(f32[4,6,96,256]{3,2,1,0:T(8,128)} %param.7) | copy-start | bytes 7077892
  428.7 313.0 %all-gather.3.cloned.1.call-start = ((), (), s32[]{:S(2)}) async-start(), calls=%async_computation.2 | async-start | bytes 4866048 | tf_op jit(solution)/shard_map/all_gather | solution.py:74
Sparse Core Ops, SparseCore 0:
  428.8 151.0 all-reduce.1
  585.6 155.9 all-gather.2
where the time goes:
time: 762 us; the launch traced here: 755 us
  waiting for transfers between devices  564 us (74%)
  matrix products  77.4 us (10%)
  local copies, waits for them, and re-layouts  62.4 us (8%)
  other arithmetic  26.5 us (3%)
  between operations  14.7 us (2%)
  starting transfers between devices  9.52 us (1%)
    all_to_all x1, waiting for transfers between devices, local(): lax.all_to_all(buffer, 'member', split_axis=0, concat_axis=0, tiled=True)  257 us
    all_gather x1, waiting for transfers between devices, local(): lax.all_gather(scaled.reshape(sub_count, prim_count * prim_count), 'membe...  156 us
    psum x1, waiting for transfers between devices, assemble_diagonal(): return lax.psum(local_diagonal, ('group', 'member'))  151 us
    dot_general x2, matrix products, inverse_sweeps(): jnp.einsum('fij,fjk->fik', summed, current, precision=FULL_PRECISION)  27.8 us
    dot_general x2, matrix products, inverse_sweeps(): jnp.einsum('fij,fjk->fik', current, doubled - applied, precision=FULL_PRE...  26.8 us
    scatter x1, local copies, waits for them, and re-layouts, local(): buffer = jnp.zeros((members, capacity) + stacked.shape[1:], jnp.float32)....  23 us
  transfers between devices with their start and end apart: 3, of which 3 were waited for; matrix products, arithmetic and copies ran while one was open for 1% of the time, Pallas kernels for 0%

commit v1 on v0

v1 whole, which is shorter than its diff:
```python
import jax
import jax.numpy as jnp
from jax import lax
from jax.experimental import pallas as pl
from jax.experimental.pallas import tpu as pltpu
from jax.sharding import PartitionSpec as P

AXES = ("group", "member")
COARSE_PER_SUB = 48
LANES = 128


def iotas(rows, cols):
    return (
        lax.broadcasted_iota(jnp.int32, (rows, cols), 0),
        lax.broadcasted_iota(jnp.int32, (rows, cols), 1),
    )


def halves(value):
    high = value.astype(jnp.bfloat16)
    return high, (value - high.astype(jnp.float32)).astype(jnp.bfloat16)


def dot(left, right, right_dim=0):
    dims = (((1,), (right_dim,)), ((), ()))
    rows = left[0].shape[0]
    stacked = jnp.concatenate(left, axis=0)
    first = lax.dot_general(stacked, right[0], dims, preferred_element_type=jnp.float32)
    second = lax.dot_general(left[0], right[1], dims, preferred_element_type=jnp.float32)
    return first[:rows] + (first[rows:] + second)


def pack_kernel(slot_ref, schur_ref, inverse_ref, out_ref):
    width = schur_ref.shape[1]
    schur, inverse = schur_ref[0], inverse_ref[0]
    row, col = iotas(width, width)
    packed = jnp.where(row <= col, schur, inverse)
    diagonal = jnp.sum(jnp.where(row == col, inverse, 0.0), axis=0, keepdims=True)
    parts = width // LANES
    for part in range(parts):
        lanes = slice(part * LANES, (part + 1) * LANES)
        out_ref[0, part * width : (part + 1) * width, :] = packed[:, lanes]
        out_ref[0, parts * width + part : parts * width + part + 1, :] = diagonal[:, lanes]


def pack(slots, schur, inverse, members):
    faces, width = schur.shape[:2]
    rows = width * width // LANES + 8
    block = pl.BlockSpec((1, width, width), lambda f, slot: (f, 0, 0))
    return pl.pallas_call(
        pack_kernel,
        out_shape=jax.ShapeDtypeStruct((members, rows, LANES), jnp.float32),
        grid_spec=pltpu.PrefetchScalarGridSpec(
            num_scalar_prefetch=1,
            grid=(faces,),
            in_specs=[block, block],
            out_specs=pl.BlockSpec((1, rows, LANES), lambda f, slot: (slot[f], 0, 0)),
        ),
        name="pack_faces",
    )(slots, schur, inverse)


def face_kernel(slot_ref, schur_ref, inverse_ref, basis_ref, *rest):
    per_step = schur_ref.shape[0]
    received = rest[:per_step]
    deluxe_ref, galerkin_ref, diagonal_ref = rest[per_step:]
    width = schur_ref.shape[1]
    prims = basis_ref.shape[1]
    parts = width // LANES
    steps_per_sub = 6 // per_step
    step = pl.program_id(0)
    row, col = iotas(width, width)
    total = None
    for face in range(per_step):
        mixed = jnp.concatenate(
            [received[face][0, p * width : (p + 1) * width, :] for p in range(parts)], axis=1
        )
        line = jnp.concatenate(
            [received[face][0, parts * width + p : parts * width + p + 1, :] for p in range(parts)], axis=1
        )
        turned = mixed.T
        other_schur = jnp.where(row <= col, mixed, turned)
        other_inverse = jnp.where(row > col, mixed, jnp.where(row == col, line, turned))
        schur = schur_ref[face]
        summed = halves(schur + other_schur)
        initial = halves(0.25 * (inverse_ref[face] + other_inverse))
        residual = halves(jnp.where(row == col, 1.0, 0.0) - dot(summed, initial))
        product = dot(halves(basis_ref[face]), halves(schur))
        start = dot(halves(product), initial)
        deluxe = start
        for _ in range(3):
            deluxe = start + dot(halves(deluxe), residual)
        deluxe_ref[face] = deluxe
        deluxe = halves(deluxe)
        weighted = dot(deluxe, halves(other_schur))
        block = dot(halves(weighted), deluxe, right_dim=1)
        total = block if total is None else total + block

    @pl.when(step == 0)
    def _():
        diagonal_ref[...] = jnp.zeros_like(diagonal_ref)

    @pl.when(step % steps_per_sub == 0)
    def _():
        galerkin_ref[0] = total

    @pl.when(step % steps_per_sub != 0)
    def _():
        galerkin_ref[0] += total

    @pl.when(step % steps_per_sub == steps_per_sub - 1)
    def _():
        row, col = iotas(prims, prims)
        line = jnp.sum(jnp.where(row == col, galerkin_ref[0], 0.0), axis=0, keepdims=True)
        diagonal_ref[pl.ds(step // steps_per_sub, 1), 0:prims] = line


def faces(slots, schur, inverse, basis, received, subs):
    count, width = schur.shape[:2]
    prims = basis.shape[1]
    rows = received.shape[1]
    per_step = 2
    steps_per_sub = 6 // per_step
    block = pl.BlockSpec((per_step, width, width), lambda i, slot: (i, 0, 0))
    thin = pl.BlockSpec((per_step, prims, width), lambda i, slot: (i, 0, 0))

    def incoming(offset):
        return pl.BlockSpec((1, rows, LANES), lambda i, slot: (slot[i * per_step + offset], 0, 0))

    return pl.pallas_call(
        face_kernel,
        out_shape=(
            jax.ShapeDtypeStruct((count, prims, width), jnp.float32),
            jax.ShapeDtypeStruct((subs, prims, prims), jnp.float32),
            jax.ShapeDtypeStruct((8, LANES), jnp.float32),
        ),
        grid_spec=pltpu.PrefetchScalarGridSpec(
            num_scalar_prefetch=1,
            grid=(count // per_step,),
            in_specs=[block, block, thin] + [incoming(o) for o in range(per_step)],
            out_specs=(
                thin,
                pl.BlockSpec((1, prims, prims), lambda i, slot: (i // steps_per_sub, 0, 0)),
                pl.BlockSpec((8, LANES), lambda i, slot: (0, 0)),
            ),
        ),
        name="face_terms",
    )(slots, schur, inverse, basis, *([received] * per_step))


def table_kernel(index_ref, value_ref, table_ref):
    highs = table_ref.shape[0]
    rows = index_ref.shape[0]
    step = pl.program_id(0)
    high_iota = lax.broadcasted_iota(jnp.int32, (highs, LANES), 0)
    low_iota = lax.broadcasted_iota(jnp.int32, (LANES, LANES), 0)
    dims = (((1,), (1,)), ((), ()))
    left, right = [], ([], [])
    for r in range(rows):
        index = index_ref[r : r + 1, :]
        high, low = halves(value_ref[r : r + 1, :])
        left.append(jnp.where(high_iota == index // LANES, 1.0, 0.0).astype(jnp.bfloat16))
        hit = low_iota == index % LANES
        for part, value in enumerate((high, low)):
            wide = value.astype(jnp.float32)
            right[part].append(jnp.where(hit, wide, 0.0).astype(jnp.bfloat16))
    left = jnp.concatenate(left, axis=1)
    total = sum(
        lax.dot_general(left, jnp.concatenate(part, axis=1), dims, preferred_element_type=jnp.float32)
        for part in right
    )

    @pl.when(step == 0)
    def _():
        table_ref[...] = total

    @pl.when(step != 0)
    def _():
        table_ref[...] += total


def coarse_table(indices, values, coarse):
    rows = indices.shape[0]
    per_step = 16
    block = pl.BlockSpec((per_step, LANES), lambda i: (i, 0))
    return pl.pallas_call(
        table_kernel,
        out_shape=jax.ShapeDtypeStruct((coarse // LANES, LANES), jnp.float32),
        grid=(rows // per_step,),
        in_specs=[block, block],
        out_specs=pl.BlockSpec((coarse // LANES, LANES), lambda i: (0, 0)),
        name="coarse_table",
    )(indices, values)


def scale_kernel(index_ref, table_ref, galerkin_ref, out_ref):
    subs = index_ref.shape[0]
    prims = 96
    highs = table_ref.shape[0]
    table = halves(table_ref[...])
    high_iota = lax.broadcasted_iota(jnp.int32, (highs, LANES), 0)
    low_iota = lax.broadcasted_iota(jnp.int32, (LANES, LANES), 0)
    dims = (((0,), (0,)), ((), ()))
    scales = []
    for s in range(subs):
        index = index_ref[s : s + 1, :]
        hit = jnp.where(high_iota == index // LANES, 1.0, 0.0).astype(jnp.bfloat16)
        rows = sum(lax.dot_general(part, hit, dims, preferred_element_type=jnp.float32) for part in table)
        value = jnp.sum(jnp.where(low_iota == index % LANES, rows, 0.0), axis=0, keepdims=True)
        scales.append(1.0 / jnp.sqrt(value))
    scale = jnp.concatenate(scales, axis=0)
    lane = lax.broadcasted_iota(jnp.int32, (subs, LANES), 1)
    scale = halves(jnp.where(lane < prims, scale, 0.0))
    period = 3 * LANES
    row, col = iotas(LANES, period)
    spread = jnp.where(row == col % prims, 1.0, 0.0).astype(jnp.bfloat16)
    right = sum(jnp.dot(part, spread, preferred_element_type=jnp.float32) for part in scale)
    for block in range(prims * prims // period):
        pick = jnp.where(row == col // prims + block * (period // prims), 1.0, 0.0).astype(jnp.bfloat16)
        left = sum(jnp.dot(part, pick, preferred_element_type=jnp.float32) for part in scale)
        lanes = slice(block * period, (block + 1) * period)
        half = subs // galerkin_ref.shape[0]
        for m in range(galerkin_ref.shape[0]):
            rows = slice(m * half, (m + 1) * half)
            out_ref[rows, lanes] = left[rows] * galerkin_ref[m, :, lanes] * right[rows]


def scale_blocks(indices, table, gathered):
    members, subs, size = gathered.shape
    per_step = 2
    return pl.pallas_call(
        scale_kernel,
        out_shape=jax.ShapeDtypeStruct((members * subs, size), jnp.float32),
        grid=(members // per_step,),
        in_specs=[
            pl.BlockSpec((per_step * subs, LANES), lambda i: (i, 0)),
            pl.BlockSpec(table.shape, lambda i: (0, 0)),
            pl.BlockSpec((per_step, subs, size), lambda i: (i, 0, 0)),
        ],
        out_specs=pl.BlockSpec((per_step * subs, size), lambda i: (i, 0)),
        name="scale_blocks",
    )(indices, table, gathered)


def everywhere(block):
    devices = lax.axis_size("group") * lax.axis_size("member")
    copies = jnp.broadcast_to(block[None], (devices,) + block.shape)
    return lax.all_to_all(copies, AXES, split_axis=0, concat_axis=0, tiled=True)


def local(face_schur, face_inverse, face_basis, partner, prim_index):
    subs, _, prims, width = face_basis.shape
    count = subs * 6
    members = lax.axis_size("member")
    groups = lax.axis_size("group")
    schur = face_schur.reshape(count, width, width)
    inverse = face_inverse.reshape(count, width, width)
    basis = face_basis.reshape(count, prims, width)
    slots = partner.reshape(count) // count % members
    padded_index = jnp.pad(prim_index, ((0, 0), (0, LANES - prims)), constant_values=-1)
    indices = everywhere(padded_index).reshape(groups * members * subs, LANES)
    sent = pack(slots, schur, inverse, members)
    received = lax.all_to_all(sent, "member", split_axis=0, concat_axis=0, tiled=True)
    deluxe, galerkin, diagonal = faces(slots, schur, inverse, basis, received, subs)
    values = everywhere(diagonal[:subs]).reshape(groups * members * subs, LANES)
    flat = galerkin.reshape(subs, prims * prims)
    gathered = lax.all_to_all(
        jnp.broadcast_to(flat[None], (members,) + flat.shape),
        "member", split_axis=0, concat_axis=0, tiled=True,
    )
    table = coarse_table(indices, values, COARSE_PER_SUB * subs * groups * members)
    start = lax.axis_index("group") * members * subs
    own = lax.dynamic_slice_in_dim(indices, start, members * subs, axis=0)
    blocks = scale_blocks(own, table, gathered)
    return deluxe.reshape(face_basis.shape), blocks


def solution(mesh):
    split = P(AXES, None, None, None)
    in_specs = (split, split, split, P(AXES, None), P(AXES, None))
    out_specs = (split, P("group", None))
    return jax.shard_map(local, mesh=mesh, in_specs=in_specs, out_specs=out_specs, check_vma=False)
```

time: 762 us -> 319 us (0.42)
  waiting for transfers between devices: 564 us -> 169 us
  Pallas kernels: 0 us -> 97.8 us
  matrix products: 77.4 us -> 0 us
  local copies, waits for them, and re-layouts: 62.4 us -> 7.4 us
  starting transfers between devices: 9.52 us -> 39.9 us
  other arithmetic: 26.5 us -> 1.99 us
  between operations: 14.7 us -> 0.7 us
    all_gather x1 -> x0, waiting for transfers between devices: 156 us -> none  [local(): lax.all_gather(scaled.reshape(sub_count, prim_count * prim_count), 'membe...]
    psum x1 -> x0, waiting for transfers between devices: 151 us -> none  [assemble_diagonal(): return lax.psum(local_diagonal, ('group', 'member'))]
    pallas_call x0 -> x4, Pallas kernels: none -> 97.8 us  [the longest x1 33.7 us: faces(): pl.pallas_call(face_kernel, out_shape=(jax.ShapeDtypeStruct((count, prims...]
    all_to_all x1 -> x4, waiting for transfers between devices: 257 us -> 169 us  [the longest x1 119 us: local(): lax.all_to_all(sent, 'member', split_axis=0, concat_axis=0, tiled=True)]
    dot_general x8 -> x0, matrix products: 77.4 us -> none  [the longest x2 27.8 us: inverse_sweeps(): jnp.einsum('fij,fjk->fik', summed, current, precision=FULL_PRECISION)]
    all_to_all x1 -> x4, starting transfers between devices: 9.44 us -> 39.9 us  [the longest x2 25.6 us: everywhere(): return lax.all_to_all(copies, AXES, split_axis=0, concat_axis=0, tiled=True)]
    scatter x1 -> x0, local copies, waits for them, and re-layouts: 23 us -> none  [local(): buffer = jnp.zeros((members, capacity) + stacked.shape[1:], jnp.float32)....]
    gather x4 -> x0, local copies, waits for them, and re-layouts: 19.7 us -> none  [the longest x1 13.1 us: local(): picked = received[target_member, recv_rank]]
  transfers between devices with their start and end apart: 3 -> 4, of which waited for: 3 -> 3; matrix products, arithmetic and copies ran while one was open for 1% -> 1% of each run, Pallas kernels for 0% -> 18%
where the time goes in v1:
time: 319 us; the launch traced here: 317 us
  waiting for transfers between devices  169 us (53%)
  Pallas kernels  97.8 us (31%)
  starting transfers between devices  39.9 us (13%)
  local copies, waits for them, and re-layouts  7.4 us (2%)
    all_to_all x1, waiting for transfers between devices, local(): lax.all_to_all(sent, 'member', split_axis=0, concat_axis=0, tiled=True)  119 us
    all_to_all x1, waiting for transfers between devices, local(): lax.all_to_all(jnp.broadcast_to(flat[None], (members,) + flat.shape), 'me...  40.2 us
    pallas_call x1, Pallas kernels, faces(): pl.pallas_call(face_kernel, out_shape=(jax.ShapeDtypeStruct((count, prims...  33.7 us
    all_to_all x2, starting transfers between devices, everywhere(): return lax.all_to_all(copies, AXES, split_axis=0, concat_axis=0, tiled=True)  25.6 us
    pallas_call x1, Pallas kernels, scale_blocks(): pl.pallas_call(scale_kernel, out_shape=jax.ShapeDtypeStruct((members * su...  25.2 us
    pallas_call x1, Pallas kernels, coarse_table(): pl.pallas_call(table_kernel, out_shape=jax.ShapeDtypeStruct((coarse // LA...  22.3 us
    pallas_call x1, Pallas kernels, pack(): pl.pallas_call(pack_kernel, out_shape=jax.ShapeDtypeStruct((members, rows...  16.5 us
    all_to_all x2, waiting for transfers between devices, everywhere(): return lax.all_to_all(copies, AXES, split_axis=0, concat_axis=0, tiled=True)  9.6 us
  transfers between devices with their start and end apart: 4, of which 3 were waited for; matrix products, arithmetic and copies ran while one was open for 1% of the time, Pallas kernels for 18%

profile of v1, /device:TPU:0, one launch (start us, length us, event | category | flops | bytes accessed | tf_op | source)
XLA Modules:
  0.0 316.6 jit_solution(11396165382045687186)
XLA Ops:
  0.6 0.7 broadcast_divide_fusion
  1.3 0.7 fusion
  2.0 0.1 div.10
  2.1 0.1 and.14
  2.2 0.6 and_select_fusion.slot_ref
  2.8 16.5 %pack_faces.1 = f32[32,520,128]{2,1,0:T(8,128)} custom-call(s32[24]{0:T(128)} %and_select_fusion.slot_ref, f32[24,256,256]{2,1,0:T(8,128)} %bitcast.6, f32[24,256,256]{2,1,0:T(8,128)} %bitcast.8), custom_call_target="tpu_custom_call" | custom-call | tf_op jit(solution)/shard_map/pack_faces/pallas_call | solution.py:51
  19.3 9.5 %all-to-all-start = ((f32[32,520,128]{2,1,0:T(8,128)}), f32[32,520,128]{2,1,0:T(8,128)}, u32[]{:S(2)}, u32[]{:S(2)}) async-start(f32[32,520,128]{2,1,0:T(8,128)} %pack_faces.1), calls=%async_computation | async-start | bytes 17039360 | tf_op jit(solution)/shard_map/all_to_all | solution.py:264
  28.9 0.0 copy-done.2
  28.9 119.0 %all-to-all-done.rest_0_.rest_1_ = f32[32,520,128]{2,1,0:T(8,128)} async-done(((f32[32,520,128]{2,1,0:T(8,128)}), f32[32,520,128]{2,1,0:T(8,128)}, u32[]{:S(2)}, u32[]{:S(2)}) %all-to-all-start) | async-done | bytes 8519712 | tf_op jit(solution)/shard_map/all_to_all | solution.py:264
  147.8 0.7 broadcast_in_dim.8
  148.6 15.8 %all-to-all-start.1 = ((s32[128,4,128]{2,1,0:T(4,128)}), s32[128,4,128]{2,1,0:T(4,128)S(1)}, u32[]{:S(2)}, u32[]{:S(2)}) async-start(s32[128,4,128]{2,1,0:T(4,128)} %broadcast_in_dim.8), calls=%async_computation.1 | async-start | bytes 524288 | tf_op jit(solution)/shard_map/all_to_all | solution.py:249
  164.4 33.7 %face_terms.1 = (f32[24,96,256]{2,1,0:T(8,128)}, f32[4,96,96]{2,1,0:T(8,128)}, f32[8,128]{1,0:T(8,128)}) custom-call(s32[24]{0:T(128)} %and_select_fusion.slot_ref, f32[24,256,256]{2,1,0:T(8,128)} %bitcast.7, f32[24,256,256]{2,1,0:T(8,128)} %bitcast.9, f32[24,96,256]{2,1,0:T(8,128)} %bitcast.10, f32[32,520,128]{2,1,0:T(8,128)} %all-to-all-done.rest_0_.rest_1_, ...), custom_call_target="tpu_custom_call" | custom-call | tf_op jit(solution)/shard_map/face_terms/pallas_call | solution.py:131
  198.1 0.7 slice.3
  198.8 0.0 all-to-all-done.1
  198.8 0.8 broadcast_in_dim.9
  199.6 9.8 %all-to-all-start.2 = ((f32[128,4,128]{2,1,0:T(4,128)}), f32[128,4,128]{2,1,0:T(4,128)S(1)}, u32[]{:S(2)}, u32[]{:S(2)}) async-start(f32[128,4,128]{2,1,0:T(4,128)} %broadcast_in_dim.9), calls=%async_computation.2 | async-start | bytes 524288 | tf_op jit(solution)/shard_map/all_to_all | solution.py:249
  209.3 1.1 broadcast_in_dim.10
  210.5 9.6 %all-to-all-done.2 = f32[128,4,128]{2,1,0:T(4,128)S(1)} async-done(((f32[128,4,128]{2,1,0:T(4,128)}), f32[128,4,128]{2,1,0:T(4,128)S(1)}, u32[]{:S(2)}, u32[]{:S(2)}) %all-to-all-start.2) | async-done | bytes 262176 | tf_op jit(solution)/shard_map/all_to_all | solution.py:249
  220.1 3.2 %broadcast_in_dim.22 = f32[32,4,9216]{2,1,0:T(4,128)} broadcast(f32[4,9216]{1,0:T(4,128)S(1)} %broadcast_in_dim.10), dimensions={1,2} | broadcast | bytes 4866048 | tf_op jit(solution)/shard_map/broadcast_in_dim | solution.py:269
  223.3 4.9 %all-to-all-start.3 = ((f32[32,4,9216]{2,1,0:T(4,128)}), f32[32,4,9216]{2,1,0:T(4,128)}, u32[]{:S(2)}, u32[]{:S(2)}) async-start(f32[32,4,9216]{2,1,0:T(4,128)} %broadcast_in_dim.22), calls=%async_computation.3 | async-start | bytes 9437184 | tf_op jit(solution)/shard_map/all_to_all | solution.py:268
  228.2 0.6 constant_dynamic-slice_fusion.index_ref
  228.8 22.3 %coarse_table.1.table_ref = f32[192,128]{1,0:T(8,128)} custom-call(s32[512,128]{1,0:T(8,128)} %bitcast.12, f32[512,128]{1,0:T(8,128)} %bitcast.13), custom_call_target="tpu_custom_call" | custom-call | tf_op jit(solution)/shard_map/coarse_table/pallas_call | solution.py:187
  251.1 40.2 %all-to-all-done.3.galerkin_ref = f32[32,4,9216]{2,1,0:T(4,128)} async-done(((f32[32,4,9216]{2,1,0:T(4,128)}), f32[32,4,9216]{2,1,0:T(4,128)}, u32[]{:S(2)}, u32[]{:S(2)}) %all-to-all-start.3) | async-done | bytes 4718624 | tf_op jit(solution)/shard_map/all_to_all | solution.py:268
  291.3 25.2 %scale_blocks.1 = f32[128,9216]{1,0:T(8,128)} custom-call(s32[128,128]{1,0:T(8,128)} %constant_dynamic-slice_fusion.index_ref, f32[192,128]{1,0:T(8,128)} %coarse_table.1.table_ref, f32[32,4,9216]{2,1,0:T(4,128)} %all-to-all-done.3.galerkin_ref), custom_call_target="tpu_custom_call" | custom-call | tf_op jit(solution)/shard_map/scale_blocks/pallas_call | solution.py:232
  (6 shorter events, 0.0 us)
Async XLA Ops:
  19.3 9.5 %copy-start.2 = (s32[4,96]{1,0:T(4,128)S(1)}, s32[4,96]{1,0:T(4,128)}, u32[]{:S(2)}) copy-start(s32[4,96]{1,0:T(4,128)} %param.9) | copy-start | bytes 4612
  19.3 128.5 %all-to-all-start = ((f32[32,520,128]{2,1,0:T(8,128)}), f32[32,520,128]{2,1,0:T(8,128)}, u32[]{:S(2)}, u32[]{:S(2)}) async-start(f32[32,520,128]{2,1,0:T(8,128)} %pack_faces.1), calls=%async_computation | async-start | bytes 17039360 | tf_op jit(solution)/shard_map/all_to_all | solution.py:264
  148.6 50.2 %all-to-all-start.1 = ((s32[128,4,128]{2,1,0:T(4,128)}), s32[128,4,128]{2,1,0:T(4,128)S(1)}, u32[]{:S(2)}, u32[]{:S(2)}) async-start(s32[128,4,128]{2,1,0:T(4,128)} %broadcast_in_dim.8), calls=%async_computation.1 | async-start | bytes 524288 | tf_op jit(solution)/shard_map/all_to_all | solution.py:249
  198.8 29.4 %copy-start = (s32[128,4,128]{2,1,0:T(4,128)}, s32[128,4,128]{2,1,0:T(4,128)S(1)}, u32[]{:S(2)}) copy-start(s32[128,4,128]{2,1,0:T(4,128)S(1)} %all-to-all-done.1) | copy-start | bytes 786436
  199.6 20.5 %all-to-all-start.2 = ((f32[128,4,128]{2,1,0:T(4,128)}), f32[128,4,128]{2,1,0:T(4,128)S(1)}, u32[]{:S(2)}, u32[]{:S(2)}) async-start(f32[128,4,128]{2,1,0:T(4,128)} %broadcast_in_dim.9), calls=%async_computation.2 | async-start | bytes 524288 | tf_op jit(solution)/shard_map/all_to_all | solution.py:249
  220.1 3.3 %copy-start.1 = (f32[128,4,128]{2,1,0:T(4,128)}, f32[128,4,128]{2,1,0:T(4,128)S(1)}, u32[]{:S(2)}) copy-start(f32[128,4,128]{2,1,0:T(4,128)S(1)} %all-to-all-done.2) | copy-start | bytes 786436
  223.3 68.0 %all-to-all-start.3 = ((f32[32,4,9216]{2,1,0:T(4,128)}), f32[32,4,9216]{2,1,0:T(4,128)}, u32[]{:S(2)}, u32[]{:S(2)}) async-start(f32[32,4,9216]{2,1,0:T(4,128)} %broadcast_in_dim.22), calls=%async_computation.3 | async-start | bytes 9437184 | tf_op jit(solution)/shard_map/all_to_all | solution.py:268

commit v2 on v1

v2 whole, which is shorter than its diff:
```python
import jax
import jax.numpy as jnp
from jax import lax
from jax.experimental import pallas as pl
from jax.experimental.pallas import tpu as pltpu
from jax.sharding import PartitionSpec as P

AXES = ("group", "member")
COARSE_PER_SUB = 48
LANES = 128
TAIL = 8
INDEX_ROW = 2


def iotas(rows, cols):
    return (
        lax.broadcasted_iota(jnp.int32, (rows, cols), 0),
        lax.broadcasted_iota(jnp.int32, (rows, cols), 1),
    )


def halves(value):
    high = value.astype(jnp.bfloat16)
    return high, (value - high.astype(jnp.float32)).astype(jnp.bfloat16)


def dot(left, right, right_dim=0):
    dims = (((1,), (right_dim,)), ((), ()))
    rows = left[0].shape[0]
    stacked = jnp.concatenate(left, axis=0)
    first = lax.dot_general(stacked, right[0], dims, preferred_element_type=jnp.float32)
    second = lax.dot_general(left[0], right[1], dims, preferred_element_type=jnp.float32)
    return first[:rows] + (first[rows:] + second)


def pack_kernel(slot_ref, tail_ref, schur_ref, inverse_ref, out_ref, schur_buf, inverse_buf, out_buf, schur_sem, inverse_sem, out_sem, tail_sem):
    count, width = schur_buf.shape[:2]
    members = out_ref.shape[0]
    parts = width // LANES
    body = parts * width

    def load(f):
        return (
            pltpu.make_async_copy(schur_ref.at[f], schur_buf.at[f], schur_sem.at[f]),
            pltpu.make_async_copy(inverse_ref.at[f], inverse_buf.at[f], inverse_sem.at[f]),
        )

    def tail(j):
        return pltpu.make_async_copy(tail_ref, out_ref.at[j, pl.ds(body, TAIL), :], tail_sem.at[j])

    def save(f):
        return pltpu.make_async_copy(out_buf.at[f], out_ref.at[slot_ref[f]], out_sem.at[f])

    for f in range(count):
        for copy in load(f):
            copy.start()
    for j in range(members):
        tail(j).start()
    for j in range(members):
        tail(j).wait()
    row, col = iotas(width, width)
    upper, middle = row <= col, row == col

    @pl.loop(0, count)
    def _(f):
        for copy in load(f):
            copy.wait()
        schur, inverse = schur_buf[f], inverse_buf[f]
        packed = jnp.where(upper, schur, inverse)
        diagonal = jnp.sum(jnp.where(middle, inverse, 0.0), axis=0, keepdims=True)
        for part in range(parts):
            lanes = slice(part * LANES, (part + 1) * LANES)
            out_buf[f, part * width : (part + 1) * width, :] = packed[:, lanes]
        out_buf[f, body : body + TAIL, :] = tail_ref[...]
        for part in range(parts):
            lanes = slice(part * LANES, (part + 1) * LANES)
            out_buf[f, body + part : body + part + 1, :] = diagonal[:, lanes]
        save(f).start()

    for f in range(count):
        save(f).wait()


def pack(slots, tail, schur, inverse, members):
    count, width = schur.shape[:2]
    rows = width * width // LANES + TAIL
    return pl.pallas_call(
        pack_kernel,
        out_shape=jax.ShapeDtypeStruct((members, rows, LANES), jnp.float32),
        in_specs=[
            pl.BlockSpec(memory_space=pltpu.SMEM),
            pl.BlockSpec(memory_space=pltpu.VMEM),
            pl.BlockSpec(memory_space=pl.ANY),
            pl.BlockSpec(memory_space=pl.ANY),
        ],
        out_specs=pl.BlockSpec(memory_space=pl.ANY),
        scratch_shapes=[
            pltpu.VMEM((count, width, width), jnp.float32),
            pltpu.VMEM((count, width, width), jnp.float32),
            pltpu.VMEM((count, rows, LANES), jnp.float32),
            pltpu.SemaphoreType.DMA((count,)),
            pltpu.SemaphoreType.DMA((count,)),
            pltpu.SemaphoreType.DMA((count,)),
            pltpu.SemaphoreType.DMA((members,)),
        ],
        name="pack_faces",
    )(slots, tail, schur, inverse)


def fold(block):
    half = block.shape[0] // 2
    row, col = iotas(half, 2 * half)
    swung = jnp.concatenate([block[half:, :half], block[:half, :half]], axis=1)
    return jnp.where((col < half) | (row > col - half), swung, block[half:, :])


def face_kernel(slot_ref, schur_ref, inverse_ref, basis_ref, *rest):
    per_step = schur_ref.shape[0]
    received = rest[:per_step]
    deluxe_ref, payload_ref, galerkin_ref = rest[per_step:]
    width = schur_ref.shape[1]
    prims = basis_ref.shape[1]
    subs = galerkin_ref.shape[0]
    parts = width // LANES
    body = parts * width
    steps_per_sub = 6 // per_step
    step = pl.program_id(0)
    every = range(per_step)
    row, col = iotas(width, width)
    other_schur, summed, initial = [], [], []
    for f in every:
        mixed = jnp.concatenate([received[f][0, p * width : (p + 1) * width, :] for p in range(parts)], axis=1)
        line = jnp.concatenate([received[f][0, body + p : body + p + 1, :] for p in range(parts)], axis=1)
        turned = mixed.T
        other = jnp.where(row <= col, mixed, turned)
        other_inverse = jnp.where(row > col, mixed, jnp.where(row == col, line, turned))
        summed.append(halves(schur_ref[f] + other))
        initial.append(halves(0.25 * (inverse_ref[f] + other_inverse)))
        other_schur.append(halves(other))
    product = [dot(halves(basis_ref[f]), halves(schur_ref[f])) for f in every]
    residual = [halves(jnp.where(row == col, 1.0, 0.0) - dot(summed[f], initial[f])) for f in every]
    start = [dot(halves(product[f]), initial[f]) for f in every]
    deluxe = start
    for _ in range(3):
        deluxe = [start[f] + dot(halves(deluxe[f]), residual[f]) for f in every]
    for f in every:
        deluxe_ref[f] = deluxe[f]
    deluxe = [halves(d) for d in deluxe]
    weighted = [dot(deluxe[f], other_schur[f]) for f in every]
    total = sum(dot(halves(weighted[f]), deluxe[f], right_dim=1) for f in every)
    sub = step // steps_per_sub

    @pl.when(step % steps_per_sub == 0)
    def _():
        galerkin_ref[sub] = total

    @pl.when(step % steps_per_sub != 0)
    def _():
        galerkin_ref[sub] += total

    @pl.when(step == subs * steps_per_sub - 1)
    def _():
        half = prims // 2
        row, col = iotas(prims, prims)
        blocks = [galerkin_ref[s] for s in range(subs)]
        lines = [jnp.sum(jnp.where(row == col, b, 0.0), axis=0, keepdims=True) for b in blocks]
        payload_ref[:half] = jnp.concatenate([fold(b) for b in blocks], axis=1)
        line = jnp.concatenate(lines, axis=1)
        payload_ref[half:] = jnp.broadcast_to(line, (payload_ref.shape[0] - half, line.shape[1]))


def faces(slots, schur, inverse, basis, received, subs):
    count, width = schur.shape[:2]
    prims = basis.shape[1]
    rows = received.shape[1]
    per_step = 2
    block = pl.BlockSpec((per_step, width, width), lambda i, slot: (i, 0, 0))
    thin = pl.BlockSpec((per_step, prims, width), lambda i, slot: (i, 0, 0))
    payload = (prims // 2 + 8, subs * prims)

    def incoming(offset):
        return pl.BlockSpec((1, rows, LANES), lambda i, slot: (slot[i * per_step + offset], 0, 0))

    return pl.pallas_call(
        face_kernel,
        out_shape=(
            jax.ShapeDtypeStruct((count, prims, width), jnp.float32),
            jax.ShapeDtypeStruct(payload, jnp.float32),
        ),
        grid_spec=pltpu.PrefetchScalarGridSpec(
            num_scalar_prefetch=1,
            grid=(count // per_step,),
            in_specs=[block, block, thin] + [incoming(o) for o in range(per_step)],
            out_specs=(thin, pl.BlockSpec(payload, lambda i, slot: (0, 0))),
            scratch_shapes=[pltpu.VMEM((subs, prims, prims), jnp.float32)],
        ),
        name="face_terms",
    )(slots, schur, inverse, basis, *([received] * per_step))


def digits(ref, m, r):
    index = ref[m, INDEX_ROW + r : INDEX_ROW + r + 1, :].astype(jnp.int32)
    high = lax.shift_right_logical(index, 7)
    return high, index - high * LANES


def table_kernel(index_ref, line_ref, table_ref):
    members = index_ref.shape[0]
    highs = table_ref.shape[0]
    chunks = line_ref.shape[2] // LANES
    high_iota = lax.broadcasted_iota(jnp.int32, (highs, LANES), 0)
    low_iota = lax.broadcasted_iota(jnp.int32, (LANES, LANES), 0)
    dims = (((1,), (1,)), ((), ()))
    group = 4
    table_ref[...] = jnp.zeros_like(table_ref)

    @pl.loop(0, members // group)
    def _(g):
        left, right, rest = [], [], []
        for k in range(group):
            m = g * group + k
            for r in range(chunks):
                high, low = digits(index_ref, m, r)
                value = line_ref[m, 0:1, r * LANES : (r + 1) * LANES]
                coarse = value.astype(jnp.bfloat16).astype(jnp.float32)
                hit = low_iota == low
                left.append(jnp.where(high_iota == high, 1.0, 0.0).astype(jnp.bfloat16))
                right.append(jnp.where(hit, coarse, 0.0).astype(jnp.bfloat16))
                rest.append(jnp.where(hit, value - coarse, 0.0).astype(jnp.bfloat16))
        left = jnp.concatenate(left, axis=1)
        right = jnp.concatenate([jnp.concatenate(right, axis=1), jnp.concatenate(rest, axis=1)], axis=0)
        total = lax.dot_general(left, right, dims, preferred_element_type=jnp.float32)
        table_ref[...] += total[:, :LANES] + total[:, LANES:]


def group_table(received, gathered, coarse):
    members, rows = received.shape[:2]
    payload = gathered.shape[1:]
    highs = coarse // LANES
    return pl.pallas_call(
        table_kernel,
        out_shape=jax.ShapeDtypeStruct((highs, LANES), jnp.float32),
        grid=(1,),
        in_specs=[
            pl.BlockSpec((members, TAIL, LANES), lambda i: (0, rows // TAIL - 1, 0)),
            pl.BlockSpec((members, 8, payload[1]), lambda i: (0, payload[0] // 8 - 1, 0)),
        ],
        out_specs=pl.BlockSpec((highs, LANES), lambda i: (0, 0)),
        name="group_table",
    )(received, gathered)


def scale_kernel(index_ref, payload_ref, *rest):
    *table_refs, out_ref, table_buf, block_buf = rest
    members, rows, lanes = payload_ref.shape
    subs = out_ref.shape[0] // members
    half = rows - 8
    prims = 2 * half
    highs = table_refs[0].shape[0]
    chunks = lanes // LANES

    @pl.when(pl.program_id(0) == 0)
    def _():
        table = sum(ref[...] for ref in table_refs).T
        high, low = halves(table)
        table_buf[:LANES] = high
        table_buf[LANES:] = low

    high_iota = lax.broadcasted_iota(jnp.int32, (highs, LANES), 0)
    low_iota = lax.broadcasted_iota(jnp.int32, (LANES, LANES), 0)
    row, col = iotas(half, prims)
    for m in range(members):
        marks, lows = [], []
        for r in range(chunks):
            high, low = digits(index_ref, m, r)
            marks.append(jnp.where(high_iota == high, 1.0, 0.0).astype(jnp.bfloat16))
            lows.append(low)
        found = jnp.dot(table_buf[...], jnp.concatenate(marks, axis=1), preferred_element_type=jnp.float32)
        found = found[:LANES] + found[LANES:]
        scale = []
        for r in range(chunks):
            hit = jnp.where(low_iota == lows[r], found[:, r * LANES : (r + 1) * LANES], 0.0)
            scale.append(1.0 / jnp.sqrt(jnp.sum(hit, axis=0, keepdims=True)))
        scale = jnp.concatenate(scale, axis=1)
        main = payload_ref[m, :half, :]
        line = payload_ref[m, half : half + 1, :]
        both = jnp.concatenate([main, jnp.broadcast_to(scale, (8, lanes))], axis=0)
        turned = both.T
        for s in range(subs):
            mine = slice(s * prims, (s + 1) * prims)
            flat, mirror = main[:, mine], turned[mine]
            line_s, scale_s = line[:, mine], scale[:, mine]
            column = mirror[:, half : half + 1]
            corner, corner_turned = flat[:, half:], mirror[half:, :half]
            top_corner = jnp.concatenate([corner, mirror[:half, :half]], axis=1)
            top_other = jnp.concatenate([corner_turned, mirror[:half, :half]], axis=1)
            top = jnp.where((row > col) | (col >= half), top_corner, jnp.where(row == col, line_s, top_other))
            low_other = jnp.concatenate([flat[:, :half], corner_turned], axis=1)
            low = jnp.where((row < col - half) | (col < half), flat, jnp.where(row == col - half, line_s, low_other))
            at = (m * subs + s) * prims
            block_buf[at : at + half, :prims] = column[:half] * top * scale_s
            block_buf[at + half : at + prims, :prims] = column[half:] * low * scale_s
    count = members * subs
    span = 4
    for a in range(0, prims, span):
        pieces = [block_buf[pl.ds(a + k, count, stride=prims), :][:, :prims] for k in range(span)]
        out_ref[:, a * prims : (a + span) * prims] = jnp.concatenate(pieces, axis=1)


def scale_blocks(received, gathered, tables, subs):
    members, rows = received.shape[:2]
    payload = gathered.shape[1:]
    prims = payload[1] // subs
    highs = tables[0].shape[0]
    per_step = 2
    whole = pl.BlockSpec((highs, LANES), lambda i: (0, 0))
    return pl.pallas_call(
        scale_kernel,
        out_shape=jax.ShapeDtypeStruct((members * subs, prims * prims), jnp.float32),
        grid=(members // per_step,),
        in_specs=[
            pl.BlockSpec((per_step, TAIL, LANES), lambda i: (i, rows // TAIL - 1, 0)),
            pl.BlockSpec((per_step,) + payload, lambda i: (i, 0, 0)),
        ]
        + [whole] * len(tables),
        out_specs=pl.BlockSpec((per_step * subs, prims * prims), lambda i: (i, 0)),
        scratch_shapes=[
            pltpu.VMEM((2 * LANES, highs), jnp.bfloat16),
            pltpu.VMEM((per_step * subs * prims, LANES), jnp.float32),
        ],
        name="scale_blocks",
    )(received, gathered, *tables)


def exchange(blocks):
    return lax.all_to_all(blocks, "member", split_axis=0, concat_axis=0, tiled=True)


def local(face_schur, face_inverse, face_basis, partner, prim_index):
    subs, _, prims, width = face_basis.shape
    count = subs * 6
    members = lax.axis_size("member")
    groups = lax.axis_size("group")
    schur = face_schur.reshape(count, width, width)
    inverse = face_inverse.reshape(count, width, width)
    basis = face_basis.reshape(count, prims, width)
    slots = lax.rem(lax.div(partner.reshape(count), count), members)
    tail = jnp.pad(prim_index.astype(jnp.float32).reshape(-1, LANES), ((INDEX_ROW, 3), (0, 0)))
    received = exchange(pack(slots, tail, schur, inverse, members))
    deluxe, payload = faces(slots, schur, inverse, basis, received, subs)
    gathered = exchange(jnp.broadcast_to(payload[None], (members,) + payload.shape))
    table = group_table(received, gathered, COARSE_PER_SUB * subs * groups * members)
    tables = [table] + [
        lax.ppermute(table, "group", [(i, (i + k) % groups) for i in range(groups)]) for k in range(1, groups)
    ]
    blocks = scale_blocks(received, gathered, tables, subs)
    return deluxe.reshape(face_basis.shape), blocks


def solution(mesh):
    split = P(AXES, None, None, None)
    in_specs = (split, split, split, P(AXES, None), P(AXES, None))
    out_specs = (split, P("group", None))
    return jax.shard_map(local, mesh=mesh, in_specs=in_specs, out_specs=out_specs, check_vma=False)
```

time: 319 us -> 218 us (0.68)
  waiting for transfers between devices: 169 us -> 5.73 us
  blocking collectives: 0 us -> 146 us
  Pallas kernels: 97.8 us -> 57.5 us
  starting transfers between devices: 39.9 us -> 3.01 us
  local copies, waits for them, and re-layouts: 7.4 us -> 2.48 us
    all_to_all x4 -> x0, waiting for transfers between devices: 169 us -> none  [the longest x1 119 us: local(): lax.all_to_all(sent, 'member', split_axis=0, concat_axis=0, tiled=True)]
    all_to_all x0 -> x2, blocking collectives: none -> 146 us  [exchange(): lax.all_to_all(blocks, 'member', split_axis=0, concat_axis=0, tiled=True)]
    all_to_all x4 -> x0, starting transfers between devices: 39.9 us -> none  [the longest x2 25.6 us: everywhere(): return lax.all_to_all(copies, AXES, split_axis=0, concat_axis=0, tiled=True)]
    pallas_call x1, Pallas kernels: 22.3 us -> 5.36 us  [group_table(): pl.pallas_call(table_kernel, out_shape=jax.ShapeDtypeStruct((highs, LANES...]
    pallas_call x1, Pallas kernels: 33.7 us -> 23.8 us  [faces(): pl.pallas_call(face_kernel, out_shape=(jax.ShapeDtypeStruct((count, prims...]
    pallas_call x1, Pallas kernels: 16.5 us -> 8.8 us  [pack(): pl.pallas_call(pack_kernel, out_shape=jax.ShapeDtypeStruct((members, rows...]
    ppermute x0 -> x3, waiting for transfers between devices: none -> 5.73 us  [local(): lax.ppermute(table, 'group', [(i, (i + k) % groups) for i in range(groups)])]
    pallas_call x1, Pallas kernels: 25.2 us -> 19.6 us  [scale_blocks(): pl.pallas_call(scale_kernel, out_shape=jax.ShapeDtypeStruct((members * su...]
  transfers between devices with their start and end apart: 4 -> 3, of which waited for: 3 -> 2; matrix products, arithmetic and copies ran while one was open for 1% -> 0% of each run, Pallas kernels for 18% -> 0%
where the time goes in v2:
time: 218 us; the launch traced here: 217 us
  blocking collectives  146 us (67%)
  Pallas kernels  57.5 us (26%)
  waiting for transfers between devices  5.73 us (3%)
  starting transfers between devices  3.01 us (1%)
  local copies, waits for them, and re-layouts  2.48 us (1%)
    all_to_all x2, blocking collectives, exchange(): lax.all_to_all(blocks, 'member', split_axis=0, concat_axis=0, tiled=True)  146 us
    pallas_call x1, Pallas kernels, faces(): pl.pallas_call(face_kernel, out_shape=(jax.ShapeDtypeStruct((count, prims...  23.8 us
    pallas_call x1, Pallas kernels, scale_blocks(): pl.pallas_call(scale_kernel, out_shape=jax.ShapeDtypeStruct((members * su...  19.6 us
    pallas_call x1, Pallas kernels, pack(): pl.pallas_call(pack_kernel, out_shape=jax.ShapeDtypeStruct((members, rows...  8.8 us
    ppermute x3, waiting for transfers between devices, local(): lax.ppermute(table, 'group', [(i, (i + k) % groups) for i in range(groups)])  5.73 us
    pallas_call x1, Pallas kernels, group_table(): pl.pallas_call(table_kernel, out_shape=jax.ShapeDtypeStruct((highs, LANES...  5.36 us
  transfers between devices with their start and end apart: 3, of which 2 were waited for; matrix products, arithmetic and copies ran while one was open for 0% of the time, Pallas kernels for 0%

profile of v2, /device:TPU:0, one launch (start us, length us, event | category | flops | bytes accessed | tf_op | source)
XLA Modules:
  0.0 217.4 jit_solution(17591740723109193196)
XLA Ops:
  0.6 0.7 broadcast_divide_fusion
  1.3 0.1 div.7
  1.4 0.5 compare_select_fusion.slot_ref
  1.9 0.7 convert_element_type.5
  2.6 0.1 reshape.26
  2.7 0.6 pad.4.tail_ref
  3.3 8.8 %pack_faces.1 = f32[32,520,128]{2,1,0:T(8,128)} custom-call(s32[24]{0:T(128)} %compare_select_fusion.slot_ref, f32[8,128]{1,0:T(8,128)} %pad.4.tail_ref, f32[24,256,256]{2,1,0:T(8,128)} %bitcast.4, f32[24,256,256]{2,1,0:T(8,128)} %bitcast.6), custom_call_target="tpu_custom_call" | custom-call | tf_op jit(solution)/shard_map/pack_faces/pallas_call | solution.py:87
  12.1 107.7 %all_to_all.10.rest_0_.rest_1_.index_ref = f32[32,520,128]{2,1,0:T(8,128)} all-to-all(f32[32,520,128]{2,1,0:T(8,128)} %pack_faces.1), channel_id=1, replica_groups=mesh['group'=4,'member'=32] {'member'}, dimensions={0} | all-to-all | bytes 17039360 | tf_op jit(solution)/shard_map/all_to_all | solution.py:336
  119.8 23.8 %face_terms.1 = (f32[24,96,256]{2,1,0:T(8,128)}, f32[56,384]{1,0:T(8,128)}) custom-call(s32[24]{0:T(128)} %compare_select_fusion.slot_ref, f32[24,256,256]{2,1,0:T(8,128)} %bitcast.5, f32[24,256,256]{2,1,0:T(8,128)} %bitcast.7, f32[24,96,256]{2,1,0:T(8,128)} %bitcast.8, f32[32,520,128]{2,1,0:T(8,128)} %all_to_all.10.rest_0_.rest_1_.index_ref, ...), custom_call_target="tpu_custom_call" | custom-call | tf_op jit(solution)/shard_map/face_terms/pallas_call | solution.py:184
  143.6 1.1 broadcast_in_dim.2
  144.6 38.5 %all_to_all.11.line_ref.payload_ref = f32[32,56,384]{2,1,0:T(8,128)} all-to-all(f32[32,56,384]{2,1,0:T(8,128)S(1)} %broadcast_in_dim.2), channel_id=1, replica_groups=mesh['group'=4,'member'=32] {'member'}, dimensions={0} | all-to-all | bytes 5505024 | tf_op jit(solution)/shard_map/all_to_all | solution.py:336
  183.1 5.4 %group_table.1.rest_0_ = f32[192,128]{1,0:T(8,128)} custom-call(f32[32,520,128]{2,1,0:T(8,128)} %all_to_all.10.rest_0_.rest_1_.index_ref, f32[32,56,384]{2,1,0:T(8,128)} %all_to_all.11.line_ref.payload_ref), custom_call_target="tpu_custom_call" | custom-call | tf_op jit(solution)/shard_map/group_table/pallas_call | solution.py:240
  188.5 0.0 collective-permute-start.2
  188.5 2.8 %collective-permute-start.1 = (f32[192,128]{1,0:T(8,128)}, f32[192,128]{1,0:T(8,128)S(1)}, u32[]{:S(2)}, u32[]{:S(2)}) collective-permute-start(f32[192,128]{1,0:T(8,128)} %group_table.1.rest_0_), channel_id=1, source_target_pairs={{0,64},{32,96},{64,0},{96,32},{1,65},{33,97},{65,1},{97,33},{2,66}... | collective-permute-start | bytes 294920 | tf_op jit(solution)/shard_map/ppermute | solution.py:354
  191.3 0.2 collective-permute-start
  191.5 0.0 collective-permute-done.2.rest_3_
  191.5 0.0 copy-start
  191.5 4.9 %collective-permute-done.1.rest_2_ = f32[192,128]{1,0:T(8,128)S(1)} collective-permute-done((f32[192,128]{1,0:T(8,128)}, f32[192,128]{1,0:T(8,128)S(1)}, u32[]{:S(2)}, u32[]{:S(2)}) %collective-permute-start.1) | collective-permute-done | bytes 98336 | tf_op jit(solution)/shard_map/ppermute | solution.py:354
  196.4 0.0 copy-start.1
  196.4 0.8 collective-permute-done.rest_1_
  197.2 0.0 copy-done
  197.2 0.0 copy-done.1
  197.2 0.6 copy-done.2
  197.9 19.6 %scale_blocks.1 = f32[128,9216]{1,0:T(8,128)} custom-call(f32[32,520,128]{2,1,0:T(8,128)} %all_to_all.10.rest_0_.rest_1_.index_ref, f32[32,56,384]{2,1,0:T(8,128)} %all_to_all.11.line_ref.payload_ref, f32[192,128]{1,0:T(8,128)} %group_table.1.rest_0_, f32[192,128]{1,0:T(8,128)} %copy-done.2, f32[192,128]{1,0:T(8,128)} %copy-done.1, f32[192,128]{1,0:T(8,128)} %copy-done), custom_call_target="tpu_custom_call" | custom-call | tf_op jit(solution)/shard_map/scale_blocks/pallas_call | solution.py:317
  (1 shorter events, 0.0 us)
Async XLA Ops:
  188.5 3.0 %collective-permute-start.2 = (f32[192,128]{1,0:T(8,128)}, f32[192,128]{1,0:T(8,128)S(1)}, u32[]{:S(2)}, u32[]{:S(2)}) collective-permute-start(f32[192,128]{1,0:T(8,128)} %group_table.1.rest_0_), channel_id=1, source_target_pairs={{0,96},{32,0},{64,32},{96,64},{1,97},{33,1},{65,33},{97,65},{2,98}... | collective-permute-start | bytes 294920 | tf_op jit(solution)/shard_map/ppermute | solution.py:354
  188.5 7.9 %collective-permute-start.1 = (f32[192,128]{1,0:T(8,128)}, f32[192,128]{1,0:T(8,128)S(1)}, u32[]{:S(2)}, u32[]{:S(2)}) collective-permute-start(f32[192,128]{1,0:T(8,128)} %group_table.1.rest_0_), channel_id=1, source_target_pairs={{0,64},{32,96},{64,0},{96,32},{1,65},{33,97},{65,1},{97,33},{2,66}... | collective-permute-start | bytes 294920 | tf_op jit(solution)/shard_map/ppermute | solution.py:354
  191.3 6.0 %collective-permute-start = (f32[192,128]{1,0:T(8,128)}, f32[192,128]{1,0:T(8,128)S(1)}, u32[]{:S(2)}, u32[]{:S(2)}) collective-permute-start(f32[192,128]{1,0:T(8,128)} %group_table.1.rest_0_), channel_id=1, source_target_pairs={{0,32},{32,64},{64,96},{96,0},{1,33},{33,65},{65,97},{97,1},{2,34}... | collective-permute-start | bytes 294920 | tf_op jit(solution)/shard_map/ppermute | solution.py:354
  191.5 5.7 %copy-start = (f32[192,128]{1,0:T(8,128)}, f32[192,128]{1,0:T(8,128)S(1)}, u32[]{:S(2)}) copy-start(f32[192,128]{1,0:T(8,128)S(1)} %collective-permute-done.2.rest_3_) | copy-start | bytes 294916
  196.4 0.9 copy-start.1
  197.2 0.6 copy-start.2

commit v3 on v2

--- a/solution.py
+++ b/solution.py
@@ -10,6 +10,8 @@
 LANES = 128
 TAIL = 8
 INDEX_ROW = 2
+MEMBERS = 32
+PER_STEP = 6
 
 
 def iotas(rows, cols):
@@ -33,7 +35,13 @@
     return first[:rows] + (first[rows:] + second)
 
 
-def pack_kernel(slot_ref, tail_ref, schur_ref, inverse_ref, out_ref, schur_buf, inverse_buf, out_buf, schur_sem, inverse_sem, out_sem, tail_sem):
+def slot_of(partner_ref, f):
+    subs, around = partner_ref.shape
+    target = partner_ref[f // around, f % around]
+    return lax.rem(lax.div(target, subs * around), MEMBERS)
+
+
+def pack_kernel(partner_ref, index_ref, schur_ref, inverse_ref, out_ref, tail_ref, schur_buf, inverse_buf, out_buf, schur_sem, inverse_sem, out_sem, tail_sem):
     count, width = schur_buf.shape[:2]
     members = out_ref.shape[0]
     parts = width // LANES
@@ -49,11 +57,16 @@
         return pltpu.make_async_copy(tail_ref, out_ref.at[j, pl.ds(body, TAIL), :], tail_sem.at[j])
 
     def save(f):
-        return pltpu.make_async_copy(out_buf.at[f], out_ref.at[slot_ref[f]], out_sem.at[f])
+        return pltpu.make_async_copy(out_buf.at[f], out_ref.at[slot_of(partner_ref, f)], out_sem.at[f])
 
     for f in range(count):
         for copy in load(f):
             copy.start()
+    index = index_ref[...].astype(jnp.float32)
+    tail_ref[...] = jnp.zeros_like(tail_ref)
+    rows = deal([index[k : k + 1] for k in range(index.shape[0])])
+    for r in range(len(rows)):
+        tail_ref[INDEX_ROW + r : INDEX_ROW + r + 1, :] = rows[r]
     for j in range(members):
         tail(j).start()
     for j in range(members):
@@ -81,7 +94,7 @@
         save(f).wait()
 
 
-def pack(slots, tail, schur, inverse, members):
+def pack(partner, prim_index, schur, inverse, members):
     count, width = schur.shape[:2]
     rows = width * width // LANES + TAIL
     return pl.pallas_call(
@@ -95,6 +108,7 @@
         ],
         out_specs=pl.BlockSpec(memory_space=pl.ANY),
         scratch_shapes=[
+            pltpu.VMEM((TAIL, LANES), jnp.float32),
             pltpu.VMEM((count, width, width), jnp.float32),
             pltpu.VMEM((count, width, width), jnp.float32),
             pltpu.VMEM((count, rows, LANES), jnp.float32),
@@ -104,17 +118,24 @@
             pltpu.SemaphoreType.DMA((members,)),
         ],
         name="pack_faces",
-    )(slots, tail, schur, inverse)
+    )(partner, prim_index, schur, inverse)
 
 
 def fold(block):
     half = block.shape[0] // 2
-    row, col = iotas(half, 2 * half)
-    swung = jnp.concatenate([block[half:, :half], block[:half, :half]], axis=1)
-    return jnp.where((col < half) | (row > col - half), swung, block[half:, :])
-
-
-def face_kernel(slot_ref, schur_ref, inverse_ref, basis_ref, *rest):
+    row, col = iotas(half, half)
+    corner = jnp.where(row > col, block[:half, :half], block[half:, half:])
+    return jnp.concatenate([corner, block[:half, half:]], axis=1)
+
+
+def deal(pieces):
+    extra = LANES - pieces[0].shape[1]
+    return [
+        jnp.concatenate([pieces[r], pieces[3][:, r * extra : (r + 1) * extra]], axis=1) for r in range(3)
+    ]
+
+
+def face_kernel(partner_ref, schur_ref, inverse_ref, basis_ref, *rest):
     per_step = schur_ref.shape[0]
     received = rest[:per_step]
     deluxe_ref, payload_ref, galerkin_ref = rest[per_step:]
@@ -134,12 +155,14 @@
         turned = mixed.T
         other = jnp.where(row <= col, mixed, turned)
         other_inverse = jnp.where(row > col, mixed, jnp.where(row == col, line, turned))
-        summed.append(halves(schur_ref[f] + other))
+        summed.append(schur_ref[f] + other)
         initial.append(halves(0.25 * (inverse_ref[f] + other_inverse)))
         other_schur.append(halves(other))
     product = [dot(halves(basis_ref[f]), halves(schur_ref[f])) for f in every]
-    residual = [halves(jnp.where(row == col, 1.0, 0.0) - dot(summed[f], initial[f])) for f in every]
-    start = [dot(halves(product[f]), initial[f]) for f in every]
+    both = [halves(jnp.concatenate([summed[f], product[f]], axis=0)) for f in every]
+    both = [dot(both[f], initial[f]) for f in every]
+    residual = [halves(jnp.where(row == col, 1.0, 0.0) - both[f][:width]) for f in every]
+    start = [both[f][width:] for f in every]
     deluxe = start
     for _ in range(3):
         deluxe = [start[f] + dot(halves(deluxe[f]), residual[f]) for f in every]
@@ -164,22 +187,22 @@
         row, col = iotas(prims, prims)
         blocks = [galerkin_ref[s] for s in range(subs)]
         lines = [jnp.sum(jnp.where(row == col, b, 0.0), axis=0, keepdims=True) for b in blocks]
-        payload_ref[:half] = jnp.concatenate([fold(b) for b in blocks], axis=1)
-        line = jnp.concatenate(lines, axis=1)
+        payload_ref[:half] = jnp.concatenate(deal([fold(b) for b in blocks]), axis=1)
+        line = jnp.concatenate(deal(lines), axis=1)
         payload_ref[half:] = jnp.broadcast_to(line, (payload_ref.shape[0] - half, line.shape[1]))
 
 
-def faces(slots, schur, inverse, basis, received, subs):
+def faces(partner, schur, inverse, basis, received, subs):
     count, width = schur.shape[:2]
     prims = basis.shape[1]
     rows = received.shape[1]
-    per_step = 2
-    block = pl.BlockSpec((per_step, width, width), lambda i, slot: (i, 0, 0))
-    thin = pl.BlockSpec((per_step, prims, width), lambda i, slot: (i, 0, 0))
+    per_step = PER_STEP
+    block = pl.BlockSpec((per_step, width, width), lambda i, partner: (i, 0, 0))
+    thin = pl.BlockSpec((per_step, prims, width), lambda i, partner: (i, 0, 0))
     payload = (prims // 2 + 8, subs * prims)
 
     def incoming(offset):
-        return pl.BlockSpec((1, rows, LANES), lambda i, slot: (slot[i * per_step + offset], 0, 0))
+        return pl.BlockSpec((1, rows, LANES), lambda i, partner: (slot_of(partner, i * per_step + offset), 0, 0))
 
     return pl.pallas_call(
         face_kernel,
@@ -191,11 +214,11 @@
             num_scalar_prefetch=1,
             grid=(count // per_step,),
             in_specs=[block, block, thin] + [incoming(o) for o in range(per_step)],
-            out_specs=(thin, pl.BlockSpec(payload, lambda i, slot: (0, 0))),
+            out_specs=(thin, pl.BlockSpec(payload, lambda i, partner: (0, 0))),
             scratch_shapes=[pltpu.VMEM((subs, prims, prims), jnp.float32)],
         ),
         name="face_terms",
-    )(slots, schur, inverse, basis, *([received] * per_step))
+    )(partner, schur, inverse, basis, *([received] * per_step))
 
 
 def digits(ref, m, r):
@@ -268,7 +291,7 @@
 
     high_iota = lax.broadcasted_iota(jnp.int32, (highs, LANES), 0)
     low_iota = lax.broadcasted_iota(jnp.int32, (LANES, LANES), 0)
-    row, col = iotas(half, prims)
+    row, col = iotas(half, LANES)
     for m in range(members):
         marks, lows = [], []
         for r in range(chunks):
@@ -281,25 +304,32 @@
         for r in range(chunks):
             hit = jnp.where(low_iota == lows[r], found[:, r * LANES : (r + 1) * LANES], 0.0)
             scale.append(1.0 / jnp.sqrt(jnp.sum(hit, axis=0, keepdims=True)))
-        scale = jnp.concatenate(scale, axis=1)
-        main = payload_ref[m, :half, :]
-        line = payload_ref[m, half : half + 1, :]
-        both = jnp.concatenate([main, jnp.broadcast_to(scale, (8, lanes))], axis=0)
-        turned = both.T
+        main, lines, turned = [], [], []
+        for r in range(chunks):
+            across = slice(r * LANES, (r + 1) * LANES)
+            main.append(payload_ref[m, :half, across])
+            lines.append(payload_ref[m, half : half + 1, across])
+            turned.append(jnp.concatenate([main[r], jnp.broadcast_to(scale[r], (8, LANES))], axis=0).T)
+
+        def gather(parts, axis):
+            parts = [lax.slice_in_dim(p, prims, LANES, axis=axis) for p in parts]
+            return jnp.concatenate(parts + [parts[0]], axis=axis)
+
         for s in range(subs):
-            mine = slice(s * prims, (s + 1) * prims)
-            flat, mirror = main[:, mine], turned[mine]
-            line_s, scale_s = line[:, mine], scale[:, mine]
-            column = mirror[:, half : half + 1]
-            corner, corner_turned = flat[:, half:], mirror[half:, :half]
-            top_corner = jnp.concatenate([corner, mirror[:half, :half]], axis=1)
-            top_other = jnp.concatenate([corner_turned, mirror[:half, :half]], axis=1)
-            top = jnp.where((row > col) | (col >= half), top_corner, jnp.where(row == col, line_s, top_other))
-            low_other = jnp.concatenate([flat[:, :half], corner_turned], axis=1)
-            low = jnp.where((row < col - half) | (col < half), flat, jnp.where(row == col - half, line_s, low_other))
+            last = s == subs - 1
+            flat = gather(main, 1) if last else main[s]
+            line = gather(lines, 1) if last else lines[s]
+            scale_s = gather(scale, 1) if last else scale[s]
+            mirror = gather(turned, 0) if last else turned[s]
+            column = mirror[:prims, half : half + 1]
+            mirror = jnp.concatenate([mirror[:prims], jnp.zeros((prims, LANES - mirror.shape[1]), jnp.float32)], axis=1)
+            top = jnp.where((col >= half) | (row > col), flat, jnp.where(row == col, line, mirror[:half]))
+            shifted = jnp.concatenate([line[:, half:], line[:, :half]], axis=1)
+            corner = jnp.where(row < col, flat, jnp.where(row == col, shifted, mirror[:half]))
+            low = jnp.concatenate([mirror[half:, :half], corner[:, : LANES - half]], axis=1)
             at = (m * subs + s) * prims
-            block_buf[at : at + half, :prims] = column[:half] * top * scale_s
-            block_buf[at + half : at + prims, :prims] = column[half:] * low * scale_s
+            block_buf[at : at + half] = column[:half] * top * scale_s
+            block_buf[at + half : at + prims] = column[half:] * low * scale_s
     count = members * subs
     span = 4
     for a in range(0, prims, span):
@@ -344,10 +374,8 @@
     schur = face_schur.reshape(count, width, width)
     inverse = face_inverse.reshape(count, width, width)
     basis = face_basis.reshape(count, prims, width)
-    slots = lax.rem(lax.div(partner.reshape(count), count), members)
-    tail = jnp.pad(prim_index.astype(jnp.float32).reshape(-1, LANES), ((INDEX_ROW, 3), (0, 0)))
-    received = exchange(pack(slots, tail, schur, inverse, members))
-    deluxe, payload = faces(slots, schur, inverse, basis, received, subs)
+    received = exchange(pack(partner, prim_index, schur, inverse, members))
+    deluxe, payload = faces(partner, schur, inverse, basis, received, subs)
     gathered = exchange(jnp.broadcast_to(payload[None], (members,) + payload.shape))
     table = group_table(received, gathered, COARSE_PER_SUB * subs * groups * members)
     tables = [table] + [

time: 218 us -> 208 us (0.954)
  Pallas kernels: 57.5 us -> 50.3 us
    pallas_call x1, Pallas kernels: 23.8 us -> 18.2 us  [faces(): pl.pallas_call(face_kernel, out_shape=(jax.ShapeDtypeStruct((count, prims...]
where the time goes in v3:
time: 208 us
  blocking collectives  146 us (70%)
  Pallas kernels  50.3 us (24%)
  waiting for transfers between devices  5.73 us (3%)
  starting transfers between devices  3.3 us (2%)
    all_to_all x2, blocking collectives, exchange(): lax.all_to_all(blocks, 'member', split_axis=0, concat_axis=0, tiled=True)  146 us
    pallas_call x1, Pallas kernels, faces(): pl.pallas_call(face_kernel, out_shape=(jax.ShapeDtypeStruct((count, prims...  18.2 us
    pallas_call x1, Pallas kernels, scale_blocks(): pl.pallas_call(scale_kernel, out_shape=jax.ShapeDtypeStruct((members * su...  17.9 us
    pallas_call x1, Pallas kernels, pack(): pl.pallas_call(pack_kernel, out_shape=jax.ShapeDtypeStruct((members, rows...  8.81 us
    ppermute x3, waiting for transfers between devices, local(): lax.ppermute(table, 'group', [(i, (i + k) % groups) for i in range(groups)])  5.73 us
    pallas_call x1, Pallas kernels, group_table(): pl.pallas_call(table_kernel, out_shape=jax.ShapeDtypeStruct((highs, LANES...  5.36 us
  transfers between devices with their start and end apart: 3, of which 2 were waited for; matrix products, arithmetic and copies ran while one was open for 0% of the time, Pallas kernels for 0%

profile of v3, /device:TPU:0, one launch (start us, length us, event | category | flops | bytes accessed | tf_op | source)
XLA Modules:
  0.0 207.8 jit_solution(6837044473986116312)
XLA Ops:
  0.6 8.8 %pack_faces.1 = f32[32,520,128]{2,1,0:T(8,128)} custom-call(s32[4,6]{1,0:T(4,128)} %partner_ref.3, s32[4,96]{1,0:T(4,128)} %index_ref.1, f32[24,256,256]{2,1,0:T(8,128)} %bitcast.4, f32[24,256,256]{2,1,0:T(8,128)} %bitcast.6), custom_call_target="tpu_custom_call" | custom-call | tf_op jit(solution)/shard_map/pack_faces/pallas_call | solution.py:100
  9.4 107.7 %all_to_all.10.rest_0_.rest_1_.rest_2_.rest_3_.rest_4_.rest_5_.index_ref = f32[32,520,128]{2,1,0:T(8,128)} all-to-all(f32[32,520,128]{2,1,0:T(8,128)} %pack_faces.1), channel_id=1, replica_groups=mesh['group'=4,'member'=32] {'member'}, dimensions={0} | all-to-all | bytes 17039360 | tf_op jit(solution)/shard_map/all_to_all | solution.py:366
  117.1 18.2 %face_terms.1 = (f32[24,96,256]{2,1,0:T(8,128)}, f32[56,384]{1,0:T(8,128)}) custom-call(s32[4,6]{1,0:T(4,128)} %partner_ref.3, f32[24,256,256]{2,1,0:T(8,128)} %bitcast.5, f32[24,256,256]{2,1,0:T(8,128)} %bitcast.7, f32[24,96,256]{2,1,0:T(8,128)} %bitcast.8, f32[32,520,128]{2,1,0:T(8,128)} %all_to_all.10.rest_0_.rest_1_.rest_2_.rest_3_.rest_4_.rest_5_.index_ref, ...), custom_call_target="tpu_custom_call" | custom-call | tf_op jit(solution)/shard_map/face_terms/pallas_call | solution.py:207
  135.4 1.1 broadcast_in_dim.2
  136.4 38.4 %all_to_all.11.line_ref.payload_ref = f32[32,56,384]{2,1,0:T(8,128)} all-to-all(f32[32,56,384]{2,1,0:T(8,128)S(1)} %broadcast_in_dim.2), channel_id=1, replica_groups=mesh['group'=4,'member'=32] {'member'}, dimensions={0} | all-to-all | bytes 5505024 | tf_op jit(solution)/shard_map/all_to_all | solution.py:366
  174.8 5.4 %group_table.1.rest_0_ = f32[192,128]{1,0:T(8,128)} custom-call(f32[32,520,128]{2,1,0:T(8,128)} %all_to_all.10.rest_0_.rest_1_.rest_2_.rest_3_.rest_4_.rest_5_.index_ref, f32[32,56,384]{2,1,0:T(8,128)} %all_to_all.11.line_ref.payload_ref), custom_call_target="tpu_custom_call" | custom-call | tf_op jit(solution)/shard_map/group_table/pallas_call | solution.py:263
  180.2 0.0 collective-permute-start.2
  180.2 3.1 %collective-permute-start.1 = (f32[192,128]{1,0:T(8,128)}, f32[192,128]{1,0:T(8,128)S(1)}, u32[]{:S(2)}, u32[]{:S(2)}) collective-permute-start(f32[192,128]{1,0:T(8,128)} %group_table.1.rest_0_), channel_id=1, source_target_pairs={{0,64},{32,96},{64,0},{96,32},{1,65},{33,97},{65,1},{97,33},{2,66}... | collective-permute-start | bytes 294920 | tf_op jit(solution)/shard_map/ppermute | solution.py:382
  183.2 0.2 collective-permute-start
  183.5 0.0 collective-permute-done.2.rest_3_
  183.5 0.0 copy-start
  183.5 4.9 %collective-permute-done.1.rest_2_ = f32[192,128]{1,0:T(8,128)S(1)} collective-permute-done((f32[192,128]{1,0:T(8,128)}, f32[192,128]{1,0:T(8,128)S(1)}, u32[]{:S(2)}, u32[]{:S(2)}) %collective-permute-start.1) | collective-permute-done | bytes 98336 | tf_op jit(solution)/shard_map/ppermute | solution.py:382
  188.3 0.0 copy-start.1
  188.3 0.9 collective-permute-done.rest_1_
  189.2 0.0 copy-done
  189.2 0.0 copy-done.1
  189.2 0.0 copy-start.2
  189.2 0.6 copy-done.2
  189.8 17.9 %scale_blocks.1 = f32[128,9216]{1,0:T(8,128)} custom-call(f32[32,520,128]{2,1,0:T(8,128)} %all_to_all.10.rest_0_.rest_1_.rest_2_.rest_3_.rest_4_.rest_5_.index_ref, f32[32,56,384]{2,1,0:T(8,128)} %all_to_all.11.line_ref.payload_ref, f32[192,128]{1,0:T(8,128)} %group_table.1.rest_0_, f32[192,128]{1,0:T(8,128)} %copy-done.2, f32[192,128]{1,0:T(8,128)} %copy-done.1, ...), custom_call_target="tpu_custom_call" | custom-call | tf_op jit(solution)/shard_map/scale_blocks/pallas_call | solution.py:347
Async XLA Ops:
  180.2 3.3 %collective-permute-start.2 = (f32[192,128]{1,0:T(8,128)}, f32[192,128]{1,0:T(8,128)S(1)}, u32[]{:S(2)}, u32[]{:S(2)}) collective-permute-start(f32[192,128]{1,0:T(8,128)} %group_table.1.rest_0_), channel_id=1, source_target_pairs={{0,96},{32,0},{64,32},{96,64},{1,97},{33,1},{65,33},{97,65},{2,98}... | collective-permute-start | bytes 294920 | tf_op jit(solution)/shard_map/ppermute | solution.py:382
  180.2 8.2 %collective-permute-start.1 = (f32[192,128]{1,0:T(8,128)}, f32[192,128]{1,0:T(8,128)S(1)}, u32[]{:S(2)}, u32[]{:S(2)}) collective-permute-start(f32[192,128]{1,0:T(8,128)} %group_table.1.rest_0_), channel_id=1, source_target_pairs={{0,64},{32,96},{64,0},{96,32},{1,65},{33,97},{65,1},{97,33},{2,66}... | collective-permute-start | bytes 294920 | tf_op jit(solution)/shard_map/ppermute | solution.py:382
  183.2 6.0 %collective-permute-start = (f32[192,128]{1,0:T(8,128)}, f32[192,128]{1,0:T(8,128)S(1)}, u32[]{:S(2)}, u32[]{:S(2)}) collective-permute-start(f32[192,128]{1,0:T(8,128)} %group_table.1.rest_0_), channel_id=1, source_target_pairs={{0,32},{32,64},{64,96},{96,0},{1,33},{33,65},{65,97},{97,1},{2,34}... | collective-permute-start | bytes 294920 | tf_op jit(solution)/shard_map/ppermute | solution.py:382
  183.5 5.7 %copy-start = (f32[192,128]{1,0:T(8,128)}, f32[192,128]{1,0:T(8,128)S(1)}, u32[]{:S(2)}) copy-start(f32[192,128]{1,0:T(8,128)S(1)} %collective-permute-done.2.rest_3_) | copy-start | bytes 294916
  188.3 0.9 copy-start.1
  189.2 0.6 copy-start.2

commit v4 on v3

--- a/solution.py
+++ b/solution.py
@@ -10,6 +10,7 @@
 LANES = 128
 TAIL = 8
 INDEX_ROW = 2
+CHUNKS = 3
 MEMBERS = 32
 PER_STEP = 6
 
@@ -47,11 +48,18 @@
     parts = width // LANES
     body = parts * width
 
+    upper_half, lower_half = pl.ds(0, LANES), pl.ds(width - LANES, LANES)
+    pieces = (
+        (schur_ref, schur_buf, schur_sem, ((upper_half, slice(None)), (lower_half, lower_half))),
+        (inverse_ref, inverse_buf, inverse_sem, ((lower_half, slice(None)), (upper_half, upper_half))),
+    )
+
     def load(f):
-        return (
-            pltpu.make_async_copy(schur_ref.at[f], schur_buf.at[f], schur_sem.at[f]),
-            pltpu.make_async_copy(inverse_ref.at[f], inverse_buf.at[f], inverse_sem.at[f]),
-        )
+        return [
+            pltpu.make_async_copy(src.at[f, *part], dst.at[f, *part], sem.at[k, f])
+            for src, dst, sem, parts in pieces
+            for k, part in enumerate(parts)
+        ]
 
     def tail(j):
         return pltpu.make_async_copy(tail_ref, out_ref.at[j, pl.ds(body, TAIL), :], tail_sem.at[j])
@@ -112,8 +120,8 @@
             pltpu.VMEM((count, width, width), jnp.float32),
             pltpu.VMEM((count, width, width), jnp.float32),
             pltpu.VMEM((count, rows, LANES), jnp.float32),
-            pltpu.SemaphoreType.DMA((count,)),
-            pltpu.SemaphoreType.DMA((count,)),
+            pltpu.SemaphoreType.DMA((2, count)),
+            pltpu.SemaphoreType.DMA((2, count)),
             pltpu.SemaphoreType.DMA((count,)),
             pltpu.SemaphoreType.DMA((members,)),
         ],
@@ -187,9 +195,8 @@
         row, col = iotas(prims, prims)
         blocks = [galerkin_ref[s] for s in range(subs)]
         lines = [jnp.sum(jnp.where(row == col, b, 0.0), axis=0, keepdims=True) for b in blocks]
-        payload_ref[:half] = jnp.concatenate(deal([fold(b) for b in blocks]), axis=1)
-        line = jnp.concatenate(deal(lines), axis=1)
-        payload_ref[half:] = jnp.broadcast_to(line, (payload_ref.shape[0] - half, line.shape[1]))
+        pieces, lines = deal([fold(b) for b in blocks]), deal(lines)
+        payload_ref[...] = jnp.concatenate(pieces + lines + [lines[0]] * (TAIL - len(lines)), axis=0)
 
 
 def faces(partner, schur, inverse, basis, received, subs):
@@ -199,7 +206,7 @@
     per_step = PER_STEP
     block = pl.BlockSpec((per_step, width, width), lambda i, partner: (i, 0, 0))
     thin = pl.BlockSpec((per_step, prims, width), lambda i, partner: (i, 0, 0))
-    payload = (prims // 2 + 8, subs * prims)
+    payload = (subs * prims * prims // 2 // LANES + TAIL, LANES)
 
     def incoming(offset):
         return pl.BlockSpec((1, rows, LANES), lambda i, partner: (slot_of(partner, i * per_step + offset), 0, 0))
@@ -230,7 +237,7 @@
 def table_kernel(index_ref, line_ref, table_ref):
     members = index_ref.shape[0]
     highs = table_ref.shape[0]
-    chunks = line_ref.shape[2] // LANES
+    chunks = CHUNKS
     high_iota = lax.broadcasted_iota(jnp.int32, (highs, LANES), 0)
     low_iota = lax.broadcasted_iota(jnp.int32, (LANES, LANES), 0)
     dims = (((1,), (1,)), ((), ()))
@@ -244,7 +251,7 @@
             m = g * group + k
             for r in range(chunks):
                 high, low = digits(index_ref, m, r)
-                value = line_ref[m, 0:1, r * LANES : (r + 1) * LANES]
+                value = line_ref[m, r : r + 1, :]
                 coarse = value.astype(jnp.bfloat16).astype(jnp.float32)
                 hit = low_iota == low
                 left.append(jnp.where(high_iota == high, 1.0, 0.0).astype(jnp.bfloat16))
@@ -266,7 +273,7 @@
         grid=(1,),
         in_specs=[
             pl.BlockSpec((members, TAIL, LANES), lambda i: (0, rows // TAIL - 1, 0)),
-            pl.BlockSpec((members, 8, payload[1]), lambda i: (0, payload[0] // 8 - 1, 0)),
+            pl.BlockSpec((members, TAIL, LANES), lambda i: (0, payload[0] // TAIL - 1, 0)),
         ],
         out_specs=pl.BlockSpec((highs, LANES), lambda i: (0, 0)),
         name="group_table",
@@ -277,10 +284,10 @@
     *table_refs, out_ref, table_buf, block_buf = rest
     members, rows, lanes = payload_ref.shape
     subs = out_ref.shape[0] // members
-    half = rows - 8
+    half = (rows - TAIL) // CHUNKS
     prims = 2 * half
     highs = table_refs[0].shape[0]
-    chunks = lanes // LANES
+    chunks = CHUNKS
 
     @pl.when(pl.program_id(0) == 0)
     def _():
@@ -306,9 +313,8 @@
             scale.append(1.0 / jnp.sqrt(jnp.sum(hit, axis=0, keepdims=True)))
         main, lines, turned = [], [], []
         for r in range(chunks):
-            across = slice(r * LANES, (r + 1) * LANES)
-            main.append(payload_ref[m, :half, across])
-            lines.append(payload_ref[m, half : half + 1, across])
+            main.append(payload_ref[m, r * half : (r + 1) * half, :])
+            lines.append(payload_ref[m, chunks * half + r : chunks * half + r + 1, :])
             turned.append(jnp.concatenate([main[r], jnp.broadcast_to(scale[r], (8, LANES))], axis=0).T)
 
         def gather(parts, axis):
@@ -340,7 +346,7 @@
 def scale_blocks(received, gathered, tables, subs):
     members, rows = received.shape[:2]
     payload = gathered.shape[1:]
-    prims = payload[1] // subs
+    prims = 2 * (payload[0] - TAIL) // CHUNKS
     highs = tables[0].shape[0]
     per_step = 2
     whole = pl.BlockSpec((highs, LANES), lambda i: (0, 0))

time: 208 us -> 205 us (0.986)
    all_to_all x2, blocking collectives: 146 us -> 144 us  [exchange(): lax.all_to_all(blocks, 'member', split_axis=0, concat_axis=0, tiled=True)]
where the time goes in v4:
time: 205 us
  blocking collectives  144 us (70%)
  Pallas kernels  49.7 us (24%)
  waiting for transfers between devices  5.73 us (3%)
  starting transfers between devices  3.26 us (2%)
    all_to_all x2, blocking collectives, exchange(): lax.all_to_all(blocks, 'member', split_axis=0, concat_axis=0, tiled=True)  144 us
    pallas_call x1, Pallas kernels, faces(): pl.pallas_call(face_kernel, out_shape=(jax.ShapeDtypeStruct((count, prims...  18.3 us
    pallas_call x1, Pallas kernels, scale_blocks(): pl.pallas_call(scale_kernel, out_shape=jax.ShapeDtypeStruct((members * su...  17.9 us
    pallas_call x1, Pallas kernels, pack(): pl.pallas_call(pack_kernel, out_shape=jax.ShapeDtypeStruct((members, rows...  8.38 us
    ppermute x3, waiting for transfers between devices, local(): lax.ppermute(table, 'group', [(i, (i + k) % groups) for i in range(groups)])  5.73 us
    pallas_call x1, Pallas kernels, group_table(): pl.pallas_call(table_kernel, out_shape=jax.ShapeDtypeStruct((highs, LANES...  5.2 us
  transfers between devices with their start and end apart: 3, of which 2 were waited for; matrix products, arithmetic and copies ran while one was open for 0% of the time, Pallas kernels for 0%

profile of v4, /device:TPU:0, one launch (start us, length us, event | category | flops | bytes accessed | tf_op | source)
XLA Modules:
  0.0 204.7 jit_solution(16073970369034784230)
XLA Ops:
  0.6 8.4 %pack_faces.1 = f32[32,520,128]{2,1,0:T(8,128)} custom-call(s32[4,6]{1,0:T(4,128)} %partner_ref.3, s32[4,96]{1,0:T(4,128)} %index_ref.1, f32[24,256,256]{2,1,0:T(8,128)} %bitcast.4, f32[24,256,256]{2,1,0:T(8,128)} %bitcast.6), custom_call_target="tpu_custom_call" | custom-call | tf_op jit(solution)/shard_map/pack_faces/pallas_call | solution.py:108
  9.0 107.7 %all_to_all.10.rest_0_.rest_1_.rest_2_.rest_3_.rest_4_.rest_5_.index_ref = f32[32,520,128]{2,1,0:T(8,128)} all-to-all(f32[32,520,128]{2,1,0:T(8,128)} %pack_faces.1), channel_id=1, replica_groups=mesh['group'=4,'member'=32] {'member'}, dimensions={0} | all-to-all | bytes 17039360 | tf_op jit(solution)/shard_map/all_to_all | solution.py:372
  116.7 18.3 %face_terms.1 = (f32[24,96,256]{2,1,0:T(8,128)}, f32[152,128]{1,0:T(8,128)}) custom-call(s32[4,6]{1,0:T(4,128)} %partner_ref.3, f32[24,256,256]{2,1,0:T(8,128)} %bitcast.5, f32[24,256,256]{2,1,0:T(8,128)} %bitcast.7, f32[24,96,256]{2,1,0:T(8,128)} %bitcast.8, f32[32,520,128]{2,1,0:T(8,128)} %all_to_all.10.rest_0_.rest_1_.rest_2_.rest_3_.rest_4_.rest_5_.index_ref, ...), custom_call_target="tpu_custom_call" | custom-call | tf_op jit(solution)/shard_map/face_terms/pallas_call | solution.py:214
  135.0 1.0 broadcast_in_dim.2
  136.0 35.9 %all_to_all.11.line_ref.payload_ref = f32[32,152,128]{2,1,0:T(8,128)} all-to-all(f32[32,152,128]{2,1,0:T(8,128)S(1)} %broadcast_in_dim.2), channel_id=1, replica_groups=mesh['group'=4,'member'=32] {'member'}, dimensions={0} | all-to-all | bytes 4980736 | tf_op jit(solution)/shard_map/all_to_all | solution.py:372
  172.0 5.2 %group_table.1.rest_0_ = f32[192,128]{1,0:T(8,128)} custom-call(f32[32,520,128]{2,1,0:T(8,128)} %all_to_all.10.rest_0_.rest_1_.rest_2_.rest_3_.rest_4_.rest_5_.index_ref, f32[32,152,128]{2,1,0:T(8,128)} %all_to_all.11.line_ref.payload_ref), custom_call_target="tpu_custom_call" | custom-call | tf_op jit(solution)/shard_map/group_table/pallas_call | solution.py:270
  177.2 0.0 collective-permute-start.2
  177.2 3.0 %collective-permute-start.1 = (f32[192,128]{1,0:T(8,128)}, f32[192,128]{1,0:T(8,128)S(1)}, u32[]{:S(2)}, u32[]{:S(2)}) collective-permute-start(f32[192,128]{1,0:T(8,128)} %group_table.1.rest_0_), channel_id=1, source_target_pairs={{0,64},{32,96},{64,0},{96,32},{1,65},{33,97},{65,1},{97,33},{2,66}... | collective-permute-start | bytes 294920 | tf_op jit(solution)/shard_map/ppermute | solution.py:388
  180.2 0.2 collective-permute-start
  180.4 0.0 collective-permute-done.2.rest_3_
  180.4 0.0 copy-start
  180.4 4.9 %collective-permute-done.1.rest_2_ = f32[192,128]{1,0:T(8,128)S(1)} collective-permute-done((f32[192,128]{1,0:T(8,128)}, f32[192,128]{1,0:T(8,128)S(1)}, u32[]{:S(2)}, u32[]{:S(2)}) %collective-permute-start.1) | collective-permute-done | bytes 98336 | tf_op jit(solution)/shard_map/ppermute | solution.py:388
  185.3 0.0 copy-start.1
  185.3 0.8 collective-permute-done.rest_1_
  186.2 0.0 copy-done
  186.2 0.0 copy-done.1
  186.2 0.0 copy-start.2
  186.2 0.6 copy-done.2
  186.8 17.9 %scale_blocks.1 = f32[128,9216]{1,0:T(8,128)} custom-call(f32[32,520,128]{2,1,0:T(8,128)} %all_to_all.10.rest_0_.rest_1_.rest_2_.rest_3_.rest_4_.rest_5_.index_ref, f32[32,152,128]{2,1,0:T(8,128)} %all_to_all.11.line_ref.payload_ref, f32[192,128]{1,0:T(8,128)} %group_table.1.rest_0_, f32[192,128]{1,0:T(8,128)} %copy-done.2, f32[192,128]{1,0:T(8,128)} %copy-done.1, ...), custom_call_target="tpu_custom_call" | custom-call | tf_op jit(solution)/shard_map/scale_blocks/pallas_call | solution.py:353
Async XLA Ops:
  177.2 3.3 %collective-permute-start.2 = (f32[192,128]{1,0:T(8,128)}, f32[192,128]{1,0:T(8,128)S(1)}, u32[]{:S(2)}, u32[]{:S(2)}) collective-permute-start(f32[192,128]{1,0:T(8,128)} %group_table.1.rest_0_), channel_id=1, source_target_pairs={{0,96},{32,0},{64,32},{96,64},{1,97},{33,1},{65,33},{97,65},{2,98}... | collective-permute-start | bytes 294920 | tf_op jit(solution)/shard_map/ppermute | solution.py:388
  177.2 8.1 %collective-permute-start.1 = (f32[192,128]{1,0:T(8,128)}, f32[192,128]{1,0:T(8,128)S(1)}, u32[]{:S(2)}, u32[]{:S(2)}) collective-permute-start(f32[192,128]{1,0:T(8,128)} %group_table.1.rest_0_), channel_id=1, source_target_pairs={{0,64},{32,96},{64,0},{96,32},{1,65},{33,97},{65,1},{97,33},{2,66}... | collective-permute-start | bytes 294920 | tf_op jit(solution)/shard_map/ppermute | solution.py:388
  180.2 6.0 %collective-permute-start = (f32[192,128]{1,0:T(8,128)}, f32[192,128]{1,0:T(8,128)S(1)}, u32[]{:S(2)}, u32[]{:S(2)}) collective-permute-start(f32[192,128]{1,0:T(8,128)} %group_table.1.rest_0_), channel_id=1, source_target_pairs={{0,32},{32,64},{64,96},{96,0},{1,33},{33,65},{65,97},{97,1},{2,34}... | collective-permute-start | bytes 294920 | tf_op jit(solution)/shard_map/ppermute | solution.py:388
  180.4 5.7 %copy-start = (f32[192,128]{1,0:T(8,128)}, f32[192,128]{1,0:T(8,128)S(1)}, u32[]{:S(2)}) copy-start(f32[192,128]{1,0:T(8,128)S(1)} %collective-permute-done.2.rest_3_) | copy-start | bytes 294916
  185.3 0.9 copy-start.1
  186.2 0.6 copy-start.2
